TPU v7x, 512 devices: a whole 4x8x8 slice. The times are simulated.
512 devices in a mesh: seq: 32 (over x, z), doc: 16 (over y, core).
Axes of the slice: x: 4, y: 8, z: 8, core: 2. Of those that a mesh axis runs over, the one named last changes fastest.
Arguments:
- queries: bfloat16 [65536, 2048], P(('doc', 'seq')), parts along dimension 0, may hold values from -5 to 5
- key_rows: bfloat16 [65536, 2048], P(('doc', 'seq')), parts along dimension 0, may hold values from -5 to 5
- value_rows: bfloat16 [65536, 2048], P(('doc', 'seq')), parts along dimension 0, may hold values from -6 to 6
- out_grad: bfloat16 [65536, 2048], P(('doc', 'seq')), parts along dimension 0, may hold values from -6 to 6
- vertical: int32 [256, 6], P('doc'), parts along dimension 0, may hold values from 0 to 31, as said below
- slash_offsets: int32 [256, 6], P('doc'), parts along dimension 0, may hold values from -31 to 31, as said below
- counts: int32 [256, 2], P('doc'), parts along dimension 0, may hold values from 1 to 6, as said below
Outputs:
- query_grad: bfloat16 [65536, 2048], P(('doc', 'seq')), parts along dimension 0
- key_grad: bfloat16 [65536, 2048], P(('doc', 'seq')), parts along dimension 0
- value_grad: bfloat16 [65536, 2048], P(('doc', 'seq')), parts along dimension 0
There are 16 independent parts, one for each index of `doc`. A program takes and returns all parts, laid end to end along the dimension named above; each array names one. Nothing has to cross between parts.
Inputs may be any that keep to these rules, and one draw needn't show every extreme that they name: counts[h, 0] is 1 to 6 and counts[h, 1] is 1 to 6; some head has both at their most and some head both at 1. `vertical`: the entries of a head are distinct. `slash_offsets`: the entries of a head are distinct and slash_offsets[h, 0] is 0 for every head.
All inputs are finite; a program needn't handle non-finite values.
Results may differ from a plain program's by a relative error of at most 0.0086.
Values may be sent and summed in bfloat16 or wider, within the bound.
No kernel may reach another device: no remote copies, remote signals or barrier semaphores. Data moves between devices by JAX's collectives and lax.ppermute only.
A program may use at most 64 MiB of HBM per device.

v0:
```python
import jax
import jax.numpy as jnp
from jax import lax
from jax.sharding import PartitionSpec as P

HEADS = 16
HEAD_DIM = 128
BLK = 128


block_group = 4


def block_lists(chosen, vert_head, slash_head, count_head, nblocks):
    vert_cap = vert_head.shape[0]
    slash_cap = slash_head.shape[0]
    rows_now = chosen.shape[0]
    vert_index = jnp.broadcast_to(vert_head[None, :], (rows_now, vert_cap))
    vert_valid = jnp.broadcast_to(
        (jnp.arange(vert_cap, dtype=jnp.int32) < count_head[0])[None, :], (rows_now, vert_cap)
    )
    slash_index = chosen[:, None] - slash_head[None, :]
    inside = (slash_index >= 0) & (slash_index < nblocks)
    repeated = jnp.any(
        (vert_index[:, :, None] == slash_index[:, None, :]) & vert_valid[:, :, None], axis=1
    )
    slash_valid = (
        (jnp.arange(slash_cap, dtype=jnp.int32) < count_head[1])[None, :]
        & inside
        & jnp.logical_not(repeated)
    )
    index_table = jnp.clip(jnp.concatenate([vert_index, slash_index], axis=1), 0, nblocks - 1)
    valid_table = jnp.concatenate([vert_valid, slash_valid], axis=1)
    return (index_table, valid_table)


def owner_backward(
    q_blocks, k_blocks, v_blocks, d_blocks, vert_head, slash_head, count_head, chosen_all
):
    nblocks, blk_rows, head_dim = q_blocks.shape
    score_scale = head_dim ** (-0.5)
    vert_cap = vert_head.shape[0]
    trips = count_head[0] + count_head[1]

    def one_group(carried, chosen):
        key_acc, value_acc = carried
        index_table, valid_table = block_lists(chosen, vert_head, slash_head, count_head, nblocks)
        q_group = q_blocks[chosen]
        d_group = d_blocks[chosen]
        group_shape = (chosen.shape[0], blk_rows, 1)

        def fetch(position):
            slot_pick = jnp.where(
                position < count_head[0], position, vert_cap + position - count_head[0]
            )
            column = lax.dynamic_index_in_dim(index_table, slot_pick, 1, keepdims=False)
            usable = lax.dynamic_index_in_dim(valid_table, slot_pick, 1, keepdims=False)[
                :, None, None
            ]
            k_tile = k_blocks[column]
            v_tile = v_blocks[column]
            scores = (
                jnp.einsum("gqd,gkd->gqk", q_group, k_tile, preferred_element_type=jnp.float32)
                * score_scale
            )
            return (column, usable, k_tile, v_tile, scores)

        def row_stats(position, running):
            row_top, row_total = running
            column, usable, k_tile, v_tile, scores = fetch(position)
            new_top = jnp.maximum(
                row_top, jnp.where(usable, jnp.max(scores, axis=-1, keepdims=True), -1e30)
            )
            added = jnp.where(
                usable, jnp.sum(jnp.exp(scores - new_top), axis=-1, keepdims=True), 0.0
            )
            return (new_top, row_total * jnp.exp(row_top - new_top) + added)

        row_top, row_total = lax.fori_loop(
            0,
            trips,
            row_stats,
            (jnp.full(group_shape, -1e30, jnp.float32), jnp.zeros(group_shape, jnp.float32)),
        )

        def probs_of(scores, usable):
            return jnp.where(usable, jnp.exp(scores - row_top) / row_total, 0.0)

        def output_step(position, running):
            column, usable, k_tile, v_tile, scores = fetch(position)
            weights = probs_of(scores, usable).astype(jnp.bfloat16)
            return running + jnp.einsum(
                "gqk,gkd->gqd", weights, v_tile, preferred_element_type=jnp.float32
            )

        attended = lax.fori_loop(
            0, trips, output_step, jnp.zeros((chosen.shape[0], blk_rows, head_dim), jnp.float32)
        )
        row_delta = jnp.sum(d_group.astype(jnp.float32) * attended, axis=-1, keepdims=True)

        def grad_step(position, running):
            query_acc, key_run, value_run = running
            column, usable, k_tile, v_tile, scores = fetch(position)
            probs = probs_of(scores, usable)
            weights = probs.astype(jnp.bfloat16)
            grad_probs = jnp.einsum(
                "gqd,gkd->gqk", d_group, v_tile, preferred_element_type=jnp.float32
            )
            grad_scores = (probs * (grad_probs - row_delta)).astype(jnp.bfloat16)
            query_acc = query_acc + jnp.einsum(
                "gqk,gkd->gqd", grad_scores, k_tile, preferred_element_type=jnp.float32
            )
            key_part = (
                jnp.einsum("gqk,gqd->gkd", grad_scores, q_group, preferred_element_type=jnp.float32)
                * score_scale
            )
            value_part = jnp.einsum(
                "gqk,gqd->gkd", weights, d_group, preferred_element_type=jnp.float32
            )
            return (
                query_acc,
                key_run.at[column].add(key_part),
                value_run.at[column].add(value_part),
            )

        start_query = jnp.zeros((chosen.shape[0], blk_rows, head_dim), jnp.float32)
        query_acc, key_acc, value_acc = lax.fori_loop(
            0, trips, grad_step, (start_query, key_acc, value_acc)
        )
        return ((key_acc, value_acc), query_acc * score_scale)

    zeros_acc = jnp.zeros((nblocks, blk_rows, head_dim), jnp.float32)
    (key_acc, value_acc), query_grad = lax.scan(one_group, (zeros_acc, zeros_acc), chosen_all)
    return (query_grad.reshape(-1, blk_rows, head_dim), key_acc, value_acc)


def body(queries, key_rows, value_rows, out_grad, vertical, slash_offsets, counts):
    tokens_here = queries.shape[0]
    device_count = lax.axis_size("seq")
    device_here = lax.axis_index("seq")
    full_width = HEADS * HEAD_DIM

    def doubled(matrix):
        return jnp.repeat(matrix.reshape(tokens_here, HEADS, HEAD_DIM), 2, axis=1)

    q_owned, k_owned, v_owned, d_owned = (
        lax.all_to_all(doubled(queries), "seq", split_axis=1, concat_axis=0, tiled=True),
        lax.all_to_all(doubled(key_rows), "seq", split_axis=1, concat_axis=0, tiled=True),
        lax.all_to_all(doubled(value_rows), "seq", split_axis=1, concat_axis=0, tiled=True),
        lax.all_to_all(doubled(out_grad), "seq", split_axis=1, concat_axis=0, tiled=True),
    )
    length = tokens_here * device_count
    nblocks = length // BLK
    per_device = 2 * HEADS // device_count
    slot_index = device_here * per_device + 0
    head_index = slot_index // 2
    parity = slot_index % 2
    chosen_all = (parity + 2 * jnp.arange(nblocks // 2, dtype=jnp.int32)).reshape(-1, block_group)

    def blockwise(matrix):
        return matrix[:, 0, :].reshape(nblocks, BLK, HEAD_DIM)

    query_sel, key_acc, value_acc = owner_backward(
        blockwise(q_owned),
        blockwise(k_owned),
        blockwise(v_owned),
        blockwise(d_owned),
        vertical[head_index],
        slash_offsets[head_index],
        counts[head_index],
        chosen_all,
    )
    query_full = (
        jnp.zeros((nblocks, BLK, HEAD_DIM), jnp.float32).at[chosen_all.reshape(-1)].set(query_sel)
    )
    query_parts = [query_full.reshape(length, HEAD_DIM)]
    key_parts = [key_acc.reshape(length, HEAD_DIM)]
    value_parts = [value_acc.reshape(length, HEAD_DIM)]
    all_parts = (query_parts, key_parts, value_parts)
    stacked = [jnp.stack(member, axis=1) for member in all_parts]
    returned = (
        lax.all_to_all(stacked[0], "seq", split_axis=0, concat_axis=1, tiled=True),
        lax.all_to_all(stacked[1], "seq", split_axis=0, concat_axis=1, tiled=True),
        lax.all_to_all(stacked[2], "seq", split_axis=0, concat_axis=1, tiled=True),
    )
    results = [
        back.reshape(tokens_here, HEADS, 2, HEAD_DIM)
        .sum(axis=2)
        .astype(jnp.bfloat16)
        .reshape(tokens_here, full_width)
        for back in returned
    ]
    return (results[0], results[1], results[2])


def solution(mesh):
    return jax.shard_map(
        body,
        mesh=mesh,
        in_specs=(
            P(("doc", "seq"), None),
            P(("doc", "seq"), None),
            P(("doc", "seq"), None),
            P(("doc", "seq"), None),
            P("doc", None),
            P("doc", None),
            P("doc", None),
        ),
        out_specs=(P(("doc", "seq"), None), P(("doc", "seq"), None), P(("doc", "seq"), None)),
        check_vma=False,
    )
```

profile of v0, /device:TPU:1, one launch (start us, length us, event | category | flops | bytes accessed | tf_op | source)
XLA Modules:
  0.0 943.8 jit_solution(14872305247815273817)
XLA Ops:
  3.1 13.8 %all-to-all-start = ((bf16[128,32,128]{2,0,1:T(8,128)(2,1)}), bf16[128,32,128]{2,0,1:T(8,128)(2,1)}, u32[]{:S(2)}, u32[]{:S(2)}) async-start(bf16[128,32,128]{2,0,1:T(8,128)(2,1)} %bitcast.28), calls=%async_computation | async-start | bytes 2097152 | tf_op jit(solution)/shard_map/all_to_all | solution.py:147
  17.1 24.4 %all-to-all-done = bf16[128,32,128]{2,0,1:T(8,128)(2,1)} async-done(((bf16[128,32,128]{2,0,1:T(8,128)(2,1)}), bf16[128,32,128]{2,0,1:T(8,128)(2,1)}, u32[]{:S(2)}, u32[]{:S(2)}) %all-to-all-start) | async-done | bytes 1048608 | tf_op jit(solution)/shard_map/all_to_all | solution.py:147
  42.9 8.6 all-to-all-start.1
  51.6 24.6 %all-to-all-done.1 = bf16[128,32,128]{2,0,1:T(8,128)(2,1)S(1)} async-done(((bf16[128,32,128]{2,0,1:T(8,128)(2,1)}), bf16[128,32,128]{2,0,1:T(8,128)(2,1)S(1)}, u32[]{:S(2)}, u32[]{:S(2)}) %all-to-all-start.1) | async-done | bytes 1048608 | tf_op jit(solution)/shard_map/all_to_all | solution.py:148
  77.5 8.6 all-to-all-start.2
  86.2 24.6 %all-to-all-done.2 = bf16[128,32,128]{2,0,1:T(8,128)(2,1)} async-done(((bf16[128,32,128]{2,0,1:T(8,128)(2,1)}), bf16[128,32,128]{2,0,1:T(8,128)(2,1)}, u32[]{:S(2)}, u32[]{:S(2)}) %all-to-all-start.2) | async-done | bytes 1048608 | tf_op jit(solution)/shard_map/all_to_all | solution.py:150
  112.0 8.6 all-to-all-start.3
  123.0 22.4 %all-to-all-done.3 = bf16[128,32,128]{2,0,1:T(8,128)(2,1)} async-done(((bf16[128,32,128]{2,0,1:T(8,128)(2,1)}), bf16[128,32,128]{2,0,1:T(8,128)(2,1)}, u32[]{:S(2)}, u32[]{:S(2)}) %all-to-all-start.3) | async-done | bytes 1048608 | tf_op jit(solution)/shard_map/all_to_all | solution.py:149
  148.5 176.5 %while.53 = (s32[]{:T(128)}, f32[32,128,128]{2,1,0:T(8,128)}, f32[32,128,128]{2,1,0:T(8,128)}, f32[4,4,128,128]{3,2,1,0:T(8,128)}, s32[1,6]{1,0:T(1,128)S(1)}, /...) while((s32[]{:T(128)}, f32[32,128,128]{2,1,0:T(8,128)}, ...), condition=%wide.region_13.14_spmd, body=%wide.region_0.13_spmd.sunk | while | flops 135928128 | bytes 9762439 | solution.py:133
  152.8 3.5 while.54
  156.3 8.9 while.55
  167.2 24.6 %while.56 = (s32[]{:T(128)}, f32[4,128,128]{2,1,0:T(8,128)S(1)}, f32[32,128,128]{2,1,0:T(8,128)}, f32[32,128,128]{2,1,0:T(8,128)}, s32[]{:T(128)}, /*index=5*/s3...) while((s32[]{:T(128)}, f32[4,128,128]{2,1,0:T(8,128)S(1)}, ...), condition=%wide.region_12.12_spmd, body=%wide.region_9.11_spmd.sunk | while | flops 84673552 | bytes 5253505 | solution.py:127
  196.9 3.5 while.54
  200.4 8.9 while.55
  211.3 24.6 %while.56 = (s32[]{:T(128)}, f32[4,128,128]{2,1,0:T(8,128)S(1)}, f32[32,128,128]{2,1,0:T(8,128)}, f32[32,128,128]{2,1,0:T(8,128)}, s32[]{:T(128)}, /*index=5*/s3...) while((s32[]{:T(128)}, f32[4,128,128]{2,1,0:T(8,128)S(1)}, ...), condition=%wide.region_12.12_spmd, body=%wide.region_9.11_spmd.sunk | while | flops 84673552 | bytes 5253505 | solution.py:127
  241.0 3.5 while.54
  244.5 8.9 while.55
  255.4 24.7 %while.56 = (s32[]{:T(128)}, f32[4,128,128]{2,1,0:T(8,128)S(1)}, f32[32,128,128]{2,1,0:T(8,128)}, f32[32,128,128]{2,1,0:T(8,128)}, s32[]{:T(128)}, /*index=5*/s3...) while((s32[]{:T(128)}, f32[4,128,128]{2,1,0:T(8,128)S(1)}, ...), condition=%wide.region_12.12_spmd, body=%wide.region_9.11_spmd.sunk | while | flops 84673552 | bytes 5253505 | solution.py:127
  288.6 8.9 while.55
  299.6 24.6 %while.56 = (s32[]{:T(128)}, f32[4,128,128]{2,1,0:T(8,128)S(1)}, f32[32,128,128]{2,1,0:T(8,128)}, f32[32,128,128]{2,1,0:T(8,128)}, s32[]{:T(128)}, /*index=5*/s3...) while((s32[]{:T(128)}, f32[4,128,128]{2,1,0:T(8,128)S(1)}, ...), condition=%wide.region_12.12_spmd, body=%wide.region_9.11_spmd.sunk | while | flops 84673552 | bytes 5253505 | solution.py:127
  329.5 498.4 %all_to_all.105 = f32[4096,1,128]{2,1,0:T(1,128)} all-to-all(f32[4096,1,128]{2,1,0:T(1,128)} %bitcast.220), channel_id=1, replica_groups=mesh['seq'=32,'doc'=16] {'seq'}, dimensions={0} | all-to-all | bytes 4194304 | tf_op jit(solution)/shard_map/all_to_all | solution.py:182
  828.0 55.1 %all_to_all.106 = f32[4096,1,128]{2,1,0:T(1,128)} all-to-all(f32[4096,1,128]{2,1,0:T(1,128)S(1)} %bitcast.217), channel_id=1, replica_groups=mesh['seq'=32,'doc'=16] {'seq'}, dimensions={0} | all-to-all | bytes 4194304 | tf_op jit(solution)/shard_map/all_to_all | solution.py:183
  883.1 8.3 all-to-all-start.6
  897.5 43.2 %all-to-all-done.6 = f32[4096,1,128]{2,1,0:T(1,128)} async-done(((f32[4096,1,128]{2,1,0:T(1,128)}), f32[4096,1,128]{2,1,0:T(1,128)}, u32[]{:S(2)}, u32[]{:S(2)}) %all-to-all-start.6) | async-done | bytes 2097184 | tf_op jit(solution)/shard_map/all_to_all | solution.py:184
  (464 shorter events, 198.9 us)
Async XLA Ops:
  0.6 1.0 copy-start
  1.8 15.2 %copy-start.3 = (bf16[128,2048]{1,0:T(8,128)(2,1)S(1)}, bf16[128,2048]{1,0:T(8,128)(2,1)}, u32[]{:S(2)}) copy-start(bf16[128,2048]{1,0:T(8,128)(2,1)} %param.16) | copy-start | bytes 1572868
  3.1 38.5 %all-to-all-start = ((bf16[128,32,128]{2,0,1:T(8,128)(2,1)}), bf16[128,32,128]{2,0,1:T(8,128)(2,1)}, u32[]{:S(2)}, u32[]{:S(2)}) async-start(bf16[128,32,128]{2,0,1:T(8,128)(2,1)} %bitcast.28), calls=%async_computation | async-start | bytes 2097152 | tf_op jit(solution)/shard_map/all_to_all | solution.py:147
  17.1 34.3 %copy-start.4 = (bf16[128,2048]{1,0:T(8,128)(2,1)S(1)}, bf16[128,2048]{1,0:T(8,128)(2,1)}, u32[]{:S(2)}) copy-start(bf16[128,2048]{1,0:T(8,128)(2,1)} %param.18) | copy-start | bytes 1572868
  42.9 33.4 %all-to-all-start.1 = ((bf16[128,32,128]{2,0,1:T(8,128)(2,1)}), bf16[128,32,128]{2,0,1:T(8,128)(2,1)S(1)}, u32[]{:S(2)}, u32[]{:S(2)}) async-start(bf16[128,32,128]{2,0,1:T(8,128)(2,1)} %bitcast.33), calls=%async_computation.1 | async-start | bytes 2097152 | tf_op jit(solution)/shard_map/all_to_all | solution.py:148
  51.6 34.5 %copy-start.5 = (bf16[128,2048]{1,0:T(8,128)(2,1)S(1)}, bf16[128,2048]{1,0:T(8,128)(2,1)}, u32[]{:S(2)}) copy-start(bf16[128,2048]{1,0:T(8,128)(2,1)} %param.17) | copy-start | bytes 1572868
  77.5 33.3 %all-to-all-start.2 = ((bf16[128,32,128]{2,0,1:T(8,128)(2,1)}), bf16[128,32,128]{2,0,1:T(8,128)(2,1)}, u32[]{:S(2)}, u32[]{:S(2)}) async-start(bf16[128,32,128]{2,0,1:T(8,128)(2,1)} %bitcast.37), calls=%async_computation.2 | async-start | bytes 2097152 | tf_op jit(solution)/shard_map/all_to_all | solution.py:150
  86.2 34.4 %copy-start.6 = (s32[16,6]{0,1:T(8,128)S(1)}, s32[16,6]{0,1:T(8,128)}, u32[]{:S(2)}) copy-start(s32[16,6]{0,1:T(8,128)} %param.20) | copy-start | bytes 1156
  86.2 34.4 %copy-start.7 = (s32[16,6]{0,1:T(8,128)S(1)}, s32[16,6]{0,1:T(8,128)}, u32[]{:S(2)}) copy-start(s32[16,6]{0,1:T(8,128)} %param.19) | copy-start | bytes 1156
  86.2 34.7 %copy-start.8 = (s32[16,2]{0,1:T(2,128)S(1)}, s32[16,2]{0,1:T(2,128)}, u32[]{:S(2)}) copy-start(s32[16,2]{0,1:T(2,128)} %param.21) | copy-start | bytes 388
  112.0 33.3 %all-to-all-start.3 = ((bf16[128,32,128]{2,0,1:T(8,128)(2,1)}), bf16[128,32,128]{2,0,1:T(8,128)(2,1)}, u32[]{:S(2)}, u32[]{:S(2)}) async-start(bf16[128,32,128]{2,0,1:T(8,128)(2,1)} %bitcast.41), calls=%async_computation.3 | async-start | bytes 2097152 | tf_op jit(solution)/shard_map/all_to_all | solution.py:149
  325.0 1.6 copy-start.2
  329.5 498.4 %copy-start.1 = (f32[32,128,128]{2,1,0:T(8,128)S(1)}, f32[32,128,128]{2,1,0:T(8,128)}, u32[]{:S(2)}) copy-start(f32[32,128,128]{2,1,0:T(8,128)} %get-tuple-element.260) | copy-start | bytes 6291460
  883.1 57.7 %all-to-all-start.6 = ((f32[4096,1,128]{2,1,0:T(1,128)}), f32[4096,1,128]{2,1,0:T(1,128)}, u32[]{:S(2)}, u32[]{:S(2)}) async-start(f32[4096,1,128]{2,1,0:T(1,128)} %bitcast.218), calls=%async_computation.6 | async-start | bytes 4194304 | tf_op jit(solution)/shard_map/all_to_all | solution.py:184
where the time goes:
time: 957 us; the launch traced here: 944 us
  blocking collectives  554 us (58%)
  waiting for transfers between devices  139 us (15%)
  local copies, waits for them, and re-layouts  101 us (11%)
  other arithmetic  74 us (8%)
  starting transfers between devices  47.9 us (5%)
  matrix products  20.3 us (2%)
    all_to_all x1, blocking collectives, body(): lax.all_to_all(stacked[0], 'seq', split_axis=0, concat_axis=1, tiled=True)  498 us
    all_to_all x1, blocking collectives, body(): lax.all_to_all(stacked[1], 'seq', split_axis=0, concat_axis=1, tiled=True)  55.1 us
    all_to_all x1, waiting for transfers between devices, body(): lax.all_to_all(stacked[2], 'seq', split_axis=0, concat_axis=1, tiled=True)  43.2 us
    gather x24, local copies, waits for them, and re-layouts, fetch(): v_tile = v_blocks[column]  43.1 us
    scatter-add x12, other arithmetic, grad_step(): key_run.at[column].add(key_part)  27.7 us
    scatter-add x12, other arithmetic, grad_step(): value_run.at[column].add(value_part)  27.6 us
    all_to_all x1, waiting for transfers between devices, body(): lax.all_to_all(doubled(key_rows), 'seq', split_axis=1, concat_axis=0, til...  24.6 us
    all_to_all x1, waiting for transfers between devices, body(): lax.all_to_all(doubled(out_grad), 'seq', split_axis=1, concat_axis=0, til...  24.6 us
  transfers between devices with their start and end apart: 5, of which 5 were waited for; matrix products, arithmetic and copies ran while one was open for 1% of the time, Pallas kernels for 0%

commit v1 on v0

v1 whole, which is shorter than its diff:
```python
import functools

import jax
import jax.numpy as jnp
from jax import lax
from jax.experimental import pallas as pl
from jax.experimental.pallas import tpu as pltpu
from jax.sharding import Mesh
from jax.sharding import PartitionSpec as P

HEADS = 16
HEAD_DIM = 128
BLK = 128
NBLOCKS = 32
HALF = NBLOCKS // 2
SLOTS = 12
SCALE = HEAD_DIM ** (-0.5)
ORDER = ("zl", "x", "zh")
SWAP = [(0, 1), (1, 0)]
NEG = -1e30
VMEM_SPEC = pl.BlockSpec(memory_space=pltpu.VMEM)
SMEM_SPEC = pl.BlockSpec(memory_space=pltpu.SMEM)


def split_kernel(sc_ref, q_ref, k_ref, v_ref, d_ref, keep_ref, send_ref):
    heads_now = q_ref.shape[1] // HEAD_DIM

    def put(ref, first, second):
        for h in range(heads_now):
            cols = slice(h * HEAD_DIM, (h + 1) * HEAD_DIM)
            ref[h, 0] = first[:, cols]
            ref[h, 1] = second[:, cols]

    @pl.when(sc_ref[1] == 1)
    def _():
        put(keep_ref.at[0], q_ref, d_ref)
        put(send_ref, k_ref, v_ref)

    @pl.when(sc_ref[1] == 0)
    def _():
        put(keep_ref.at[0], k_ref, v_ref)
        put(send_ref, q_ref, d_ref)


def split_call(scalars, q, k, v, d):
    step_heads = 4
    in_spec = pl.BlockSpec((BLK, step_heads * HEAD_DIM), lambda g, sc: (0, g))
    return pl.pallas_call(
        split_kernel,
        grid_spec=pltpu.PrefetchScalarGridSpec(
            num_scalar_prefetch=1,
            grid=(HEADS // step_heads,),
            in_specs=[in_spec] * 4,
            out_specs=[
                pl.BlockSpec((1, step_heads, 2, BLK, HEAD_DIM), lambda g, sc: (sc[0], g, 0, 0, 0)),
                pl.BlockSpec((step_heads, 2, BLK, HEAD_DIM), lambda g, sc: (g, 0, 0, 0)),
            ],
        ),
        out_shape=[
            jax.ShapeDtypeStruct((2, HEADS, 2, BLK, HEAD_DIM), jnp.bfloat16),
            jax.ShapeDtypeStruct((HEADS, 2, BLK, HEAD_DIM), jnp.bfloat16),
        ],
        name="split_heads",
    )(scalars, q, k, v, d)


def attend_kernel(
    sc_ref, tab_ref, y_ref, z_ref, dq_ref, send_ref, loc_ref, kv, kt, acc, s_buf, g_buf
):
    core = sc_ref[0]

    def load_keys(t, ref, m, lead):
        k_tile = ref[lead + (m, 0)]
        kv[t, :, :HEAD_DIM] = k_tile
        kv[t, :, HEAD_DIM:] = ref[lead + (m, 1)]
        kt[t] = k_tile.T
        acc[t] = jnp.zeros((BLK, 2 * HEAD_DIM), jnp.float32)

    @pl.loop(0, HALF)
    def _(m):
        load_keys(m, z_ref, m, ())
        load_keys(HALF + m, y_ref, m, (1 - core,))

    zero = jnp.zeros((HEAD_DIM, HEAD_DIM), jnp.bfloat16)

    def diagonal(first, second):
        return jnp.concatenate(
            [jnp.concatenate([first, zero], axis=1), jnp.concatenate([zero, second], axis=1)],
            axis=0,
        )

    @pl.loop(0, HALF)
    def _(m):
        q = y_ref[core, m, 0]
        d = y_ref[core, m, 1]
        into_scores = diagonal(q.T, d.T)
        into_grads = diagonal(q, d)
        count = tab_ref[m, SLOTS]
        pairs = (count + 1) // 2

        def scores_step(g, top):
            for u in range(2):
                a = 2 * g + u
                t = tab_ref[m, a]
                both = jnp.dot(kv[t], into_scores, preferred_element_type=jnp.float32)
                s = both[:, :BLK] + jnp.where(a < count, 0.0, NEG)
                s_buf[a] = s
                g_buf[a] = both[:, BLK:]
                top = jnp.maximum(top, jnp.max(s, axis=0, keepdims=True))
            return top

        top = lax.fori_loop(0, pairs, scores_step, jnp.full((1, BLK), NEG, jnp.float32))

        def exp_step(g, sums):
            total, weighted = sums
            for u in range(2):
                a = 2 * g + u
                e = jnp.exp((s_buf[a] - top) * SCALE)
                s_buf[a] = e
                total = total + jnp.sum(e, axis=0, keepdims=True)
                weighted = weighted + jnp.sum(e * g_buf[a], axis=0, keepdims=True)
            return total, weighted

        zero_row = jnp.zeros((1, BLK), jnp.float32)
        total, weighted = lax.fori_loop(0, pairs, exp_step, (zero_row, zero_row))
        inverse = 1.0 / total
        delta = weighted * inverse

        def grad_step(g, dq_t):
            for u in range(2):
                a = 2 * g + u
                t = tab_ref[m, a]
                p = s_buf[a] * inverse
                w = p.astype(jnp.bfloat16)
                ds = (p * (g_buf[a] - delta)).astype(jnp.bfloat16)
                acc[t] += jnp.dot(
                    jnp.concatenate([ds, w], axis=1), into_grads, preferred_element_type=jnp.float32
                )
                dq_t = dq_t + jnp.dot(kt[t], ds, preferred_element_type=jnp.float32)
            return dq_t

        dq_t = lax.fori_loop(0, pairs, grad_step, jnp.zeros((HEAD_DIM, BLK), jnp.float32))
        dq_ref[m] = (dq_t * SCALE).T.astype(jnp.bfloat16)

    hb = BLK // 2

    @pl.loop(0, HALF)
    def _(m):
        near = acc[m]
        far = acc[HALF + m]
        send_ref[m, :BLK] = (near[:, :HEAD_DIM] * SCALE).astype(jnp.bfloat16)
        send_ref[m, BLK : BLK + hb] = near[hb:, HEAD_DIM:].astype(jnp.bfloat16)
        send_ref[m, BLK + hb :] = far[:hb, HEAD_DIM:].astype(jnp.bfloat16)
        loc_ref[m, :BLK] = far[:, :HEAD_DIM] * SCALE
        loc_ref[m, BLK : BLK + hb] = far[hb:, HEAD_DIM:]
        loc_ref[m, BLK + hb :] = near[:hb, HEAD_DIM:]


def attend_call(scalars, table, y, z):
    return pl.pallas_call(
        attend_kernel,
        in_specs=[SMEM_SPEC, SMEM_SPEC, VMEM_SPEC, VMEM_SPEC],
        out_specs=[VMEM_SPEC, VMEM_SPEC, VMEM_SPEC],
        out_shape=[
            jax.ShapeDtypeStruct((HALF, BLK, HEAD_DIM), jnp.bfloat16),
            jax.ShapeDtypeStruct((HALF, 2 * BLK, HEAD_DIM), jnp.bfloat16),
            jax.ShapeDtypeStruct((HALF, 2 * BLK, HEAD_DIM), jnp.float32),
        ],
        scratch_shapes=[
            pltpu.VMEM((NBLOCKS, BLK, 2 * HEAD_DIM), jnp.bfloat16),
            pltpu.VMEM((NBLOCKS, HEAD_DIM, BLK), jnp.bfloat16),
            pltpu.VMEM((NBLOCKS, BLK, 2 * HEAD_DIM), jnp.float32),
            pltpu.VMEM((SLOTS, BLK, BLK), jnp.float32),
            pltpu.VMEM((SLOTS, BLK, BLK), jnp.float32),
        ],
        compiler_params=pltpu.CompilerParams(vmem_limit_bytes=40 * 1024 * 1024),
        name="attend",
    )(scalars, table, y, z)


def join_kernel(sc_ref, dq_ref, loc_ref, got_ref, out_ref):
    core = sc_ref[0]
    hb = BLK // 2
    summed = (loc_ref[...] + got_ref[...].astype(jnp.float32)).astype(jnp.bfloat16)
    out_ref[core, :, :BLK] = dq_ref[...]
    out_ref[core, :, BLK:] = summed[:, BLK + hb :]
    out_ref[1 - core] = summed[:, : BLK + hb]


def join_call(scalars, dq, loc, got):
    return pl.pallas_call(
        join_kernel,
        in_specs=[SMEM_SPEC, VMEM_SPEC, VMEM_SPEC, VMEM_SPEC],
        out_specs=VMEM_SPEC,
        out_shape=jax.ShapeDtypeStruct((2, HALF, BLK + BLK // 2, HEAD_DIM), jnp.bfloat16),
        compiler_params=pltpu.CompilerParams(vmem_limit_bytes=40 * 1024 * 1024),
        name="join_partials",
    )(scalars, dq, loc, got)


def merge_kernel(sc_ref, own_ref, got_ref, dq_ref, dk_ref, dv_ref):
    heads_now = dq_ref.shape[1] // HEAD_DIM
    hb = BLK // 2

    def put(first, second):
        for h in range(heads_now):
            cols = slice(h * HEAD_DIM, (h + 1) * HEAD_DIM)
            dq_ref[:, cols] = first[h, :BLK]
            dv_ref[:hb, cols] = first[h, BLK:]
            dk_ref[:, cols] = second[h, :BLK]
            dv_ref[hb:, cols] = second[h, BLK:]

    @pl.when(sc_ref[1] == 1)
    def _():
        put(own_ref.at[0], got_ref)

    @pl.when(sc_ref[1] == 0)
    def _():
        put(got_ref, own_ref.at[0])


def merge_call(scalars, own, got):
    step_heads = 4
    out_spec = pl.BlockSpec((BLK, step_heads * HEAD_DIM), lambda g, sc: (0, g))
    rows = BLK + BLK // 2
    return pl.pallas_call(
        merge_kernel,
        grid_spec=pltpu.PrefetchScalarGridSpec(
            num_scalar_prefetch=1,
            grid=(HEADS // step_heads,),
            in_specs=[
                pl.BlockSpec((1, step_heads, rows, HEAD_DIM), lambda g, sc: (sc[0], g, 0, 0)),
                pl.BlockSpec((step_heads, rows, HEAD_DIM), lambda g, sc: (g, 0, 0)),
            ],
            out_specs=[out_spec] * 3,
        ),
        out_shape=[jax.ShapeDtypeStruct((BLK, HEADS * HEAD_DIM), jnp.bfloat16)] * 3,
        name="merge_heads",
    )(scalars, own, got)


def block_table(vert, slash, count, core):
    chosen = core + 2 * jnp.arange(HALF, dtype=jnp.int32)
    vert_index = jnp.broadcast_to(vert[None, :], (HALF, vert.shape[0]))
    vert_valid = jnp.broadcast_to(
        (jnp.arange(vert.shape[0], dtype=jnp.int32) < count[0])[None, :], vert_index.shape
    )
    slash_index = chosen[:, None] - slash[None, :]
    inside = (slash_index >= 0) & (slash_index < NBLOCKS)
    repeated = jnp.any(
        (vert_index[:, :, None] == slash_index[:, None, :]) & vert_valid[:, :, None], axis=1
    )
    slash_valid = (
        (jnp.arange(slash.shape[0], dtype=jnp.int32) < count[1])[None, :]
        & inside
        & jnp.logical_not(repeated)
    )
    index = jnp.concatenate([vert_index, slash_index], axis=1)
    valid = jnp.concatenate([vert_valid, slash_valid], axis=1)
    place = ((index & 1) ^ core) * HALF + (index >> 1)
    rank = jnp.cumsum(valid.astype(jnp.int32), axis=1) - 1
    lanes = jnp.arange(SLOTS, dtype=jnp.int32)
    hit = valid[:, :, None] & (rank[:, :, None] == lanes[None, None, :])
    packed = jnp.sum(jnp.where(hit, place[:, :, None], 0), axis=1)
    total = jnp.sum(valid.astype(jnp.int32), axis=1, keepdims=True)
    return jnp.concatenate([packed, total], axis=1)


def body(queries, key_rows, value_rows, out_grad, vertical, slash_offsets, counts):
    core = lax.axis_index("core")
    parity = lax.axis_index("zl")
    head = lax.axis_index("x") * lax.axis_size("zh") + lax.axis_index("zh")
    scalars = jnp.stack([core, (core == parity).astype(jnp.int32)]).astype(jnp.int32)

    tables = jnp.concatenate([vertical, slash_offsets, counts], axis=1)
    other_tables = lax.ppermute(tables, "core", SWAP)
    row = jnp.where(core == parity, tables[head], other_tables[head])
    nv, ns = vertical.shape[1], slash_offsets.shape[1]
    table = block_table(row[:nv], row[nv : nv + ns], row[nv + ns :], core)

    kept, sent = split_call(scalars, queries, key_rows, value_rows, out_grad)
    got = lax.ppermute(sent, "core", SWAP)
    kept = lax.dynamic_update_slice(kept, got[None], (1 - core, 0, 0, 0, 0))
    spread = kept.reshape(NBLOCKS, 2, BLK, HEAD_DIM)
    arrived = lax.all_to_all(spread, ORDER, split_axis=0, concat_axis=0, tiled=True)
    arrived = arrived.reshape(2, HALF, 2, BLK, HEAD_DIM)
    far_keys = lax.dynamic_index_in_dim(arrived, 1 - core, 0, keepdims=False)
    near_keys = lax.ppermute(far_keys, "core", SWAP)

    dq, partial, local = attend_call(scalars, table, arrived, near_keys)
    got_partial = lax.ppermute(partial, "core", SWAP)
    outgoing = join_call(scalars, dq, local, got_partial)
    outgoing = outgoing.reshape(NBLOCKS, BLK + BLK // 2, HEAD_DIM)
    returned = lax.all_to_all(outgoing, ORDER, split_axis=0, concat_axis=0, tiled=True)
    returned = returned.reshape(2, HALF, BLK + BLK // 2, HEAD_DIM)
    for_other = lax.dynamic_index_in_dim(returned, 1 - core, 0, keepdims=False)
    from_other = lax.ppermute(for_other, "core", SWAP)
    return tuple(merge_call(scalars, returned, from_other))


def solution(mesh):
    devices = mesh.devices
    fine = Mesh(devices.reshape(4, 4, 2, 8, 2), ("x", "zh", "zl", "y", "core"))
    rows = P(("y", "core", "x", "zh", "zl"), None)
    lists = P(("y", "core"), None)
    return jax.shard_map(
        body,
        mesh=fine,
        in_specs=(rows, rows, rows, rows, lists, lists, lists),
        out_specs=(rows, rows, rows),
        check_vma=False,
    )
```

time: 957 us -> 184 us (0.19); the launches traced: 944 us -> 183 us
  blocking collectives: 554 us -> 45.6 us
  local copies, waits for them, and re-layouts: 101 us -> 3.83 us
  waiting for transfers between devices: 139 us -> 51 us
  other arithmetic: 74 us -> 2.72 us
  Pallas kernels: 0 us -> 47.6 us
  matrix products: 20.3 us -> 0 us
  starting transfers between devices: 47.9 us -> 31.6 us
    all_to_all x2 -> x1, blocking collectives: 554 us -> 45.6 us  [body(): lax.all_to_all(outgoing, ORDER, split_axis=0, concat_axis=0, tiled=True)]
    all_to_all x5 -> x1, waiting for transfers between devices: 139 us -> 42.4 us  [body(): lax.all_to_all(spread, ORDER, split_axis=0, concat_axis=0, tiled=True)]
    gather x68 -> x0, local copies, waits for them, and re-layouts: 78.1 us -> none  [the longest x24 43.1 us: fetch(): v_tile = v_blocks[column]]
    scatter-add x24 -> x0, other arithmetic: 55.4 us -> none  [the longest x12 27.7 us: grad_step(): key_run.at[column].add(key_part)]
    pallas_call x0 -> x4, Pallas kernels: none -> 47.6 us  [the longest x1 37.8 us: attend_call(): pl.pallas_call(attend_kernel, in_specs=[SMEM_SPEC, SMEM_SPEC, VMEM_SPEC,...]
    all_to_all x5 -> x1, starting transfers between devices: 47.9 us -> 7.63 us  [body(): lax.all_to_all(spread, ORDER, split_axis=0, concat_axis=0, tiled=True)]
    ppermute x0 -> x5, starting transfers between devices: none -> 24 us  [the longest x1 8.78 us: body(): got = lax.ppermute(sent, 'core', SWAP)]
    dot_general x84 -> x0, matrix products: 20.3 us -> none  [the longest x24 5.36 us: fetch(): jnp.einsum('gqd,gkd->gqk', q_group, k_tile, preferred_element_type=jnp.fl...]
  transfers between devices with their start and end apart: 5 -> 6, of which waited for: 5 -> 6; matrix products, arithmetic and copies ran while one was open for 1% -> 2% of each run, Pallas kernels for 0% -> 0%
where the time goes in v1:
time: 184 us; the launch traced here: 183 us
  waiting for transfers between devices  51 us (28%)
  Pallas kernels  47.6 us (26%)
  blocking collectives  45.6 us (25%)
  starting transfers between devices  31.6 us (17%)
  local copies, waits for them, and re-layouts  3.83 us (2%)
  other arithmetic  2.72 us (1%)
    all_to_all x1, blocking collectives, body(): lax.all_to_all(outgoing, ORDER, split_axis=0, concat_axis=0, tiled=True)  45.6 us
    all_to_all x1, waiting for transfers between devices, body(): lax.all_to_all(spread, ORDER, split_axis=0, concat_axis=0, tiled=True)  42.4 us
    pallas_call x1, Pallas kernels, attend_call(): pl.pallas_call(attend_kernel, in_specs=[SMEM_SPEC, SMEM_SPEC, VMEM_SPEC,...  37.8 us
    ppermute x1, starting transfers between devices, body(): got = lax.ppermute(sent, 'core', SWAP)  8.78 us
    all_to_all x1, starting transfers between devices, body(): lax.all_to_all(spread, ORDER, split_axis=0, concat_axis=0, tiled=True)  7.63 us
    ppermute x1, starting transfers between devices, body(): near_keys = lax.ppermute(far_keys, 'core', SWAP)  5.75 us
    pallas_call x1, Pallas kernels, split_call(): pl.pallas_call(split_kernel, grid_spec=pltpu.PrefetchScalarGridSpec(num_s...  4.69 us
    pallas_call x1, Pallas kernels, merge_call(): pl.pallas_call(merge_kernel, grid_spec=pltpu.PrefetchScalarGridSpec(num_s...  4.37 us
  transfers between devices with their start and end apart: 6, of which 6 were waited for; matrix products, arithmetic and copies ran while one was open for 2% of the time, Pallas kernels for 0%

profile of v1, /device:TPU:1, one launch (start us, length us, event | category | flops | bytes accessed | tf_op | source)
XLA Modules:
  0.0 183.2 jit_solution(7000708064999755574)
XLA Ops:
  0.6 0.7 pad_add_fusion.4.sc_ref
  1.3 4.7 %split_heads.1 = (bf16[2,16,2,128,128]{4,3,2,1,0:T(8,128)(2,1)}, bf16[16,2,128,128]{3,2,1,0:T(8,128)(2,1)}) custom-call(s32[2]{0:T(128)} %pad_add_fusion.4.sc_ref, bf16[128,2048]{1,0:T(8,128)(2,1)} %q_ref.1, bf16[128,2048]{1,0:T(8,128)(2,1)} %k_ref.1, bf16[128,2048]{1,0:T(8,128)(2,1)} %v_ref.1, bf16[128,2048]{1,0:T(8,128)(2,1)} %d_ref.1), custom_call_target="tpu_custom_call" | custom-call | tf_op jit(solution)/shard_map/split_heads/pallas_call | solution.py:48
  6.0 8.8 %collective-permute-start.1 = (bf16[16,2,128,128]{3,2,1,0:T(8,128)(2,1)}, bf16[16,2,128,128]{3,2,1,0:T(8,128)(2,1)S(1)}, u32[]{:S(2)}, u32[]{:S(2)}) collective-permute-start(bf16[16,2,128,128]{3,2,1,0:T(8,128)(2,1)} %get-tuple-element.9), channel_id=1, source_target_pairs={{0,1},{1,0},{2,3},{3,2},{4,5},{5,4},{6,7},{7,6},{8,9},{9,8},{10,11... | collective-permute-start | bytes 3145736 | tf_op jit(solution)/shard_map/ppermute | solution.py:282
  14.8 2.5 %collective-permute-done.1 = bf16[16,2,128,128]{3,2,1,0:T(8,128)(2,1)S(1)} collective-permute-done((bf16[16,2,128,128]{3,2,1,0:T(8,128)(2,1)}, bf16[16,2,128,128]{3,2,1,0:T(8,128)(2,1)S(1)}, u32[]{:S(2)}, u32[]{:S(2)}) %collective-permute-start.1) | collective-permute-done | bytes 1048608 | tf_op jit(solution)/shard_map/ppermute | solution.py:282
  17.3 1.0 bitcast_dynamic-update-slice_fusion
  18.3 7.6 %all-to-all-start = ((bf16[32,2,128,128]{3,2,1,0:T(8,128)(2,1)}), bf16[32,2,128,128]{3,2,1,0:T(8,128)(2,1)S(1)}, u32[]{:S(2)}, u32[]{:S(2)}) async-start(bf16[32,2,128,128]{3,2,1,0:T(8,128)(2,1)} %bitcast.20), calls=%async_computation | async-start | bytes 4194304 | tf_op jit(solution)/shard_map/all_to_all | solution.py:285
  26.0 2.6 %collective-permute-start = (s32[16,14]{0,1:T(8,128)S(1)}, s32[16,14]{0,1:T(8,128)S(1)}, u32[]{:S(2)}, u32[]{:S(2)}) collective-permute-start(s32[16,14]{0,1:T(8,128)S(1)} %pad_add_fusion), channel_id=1, source_target_pairs={{0,1},{1,0},{2,3},{3,2},{4,5},{5,4},{6,7},{7,6},{8,9},{9,8},{10,11... | collective-permute-start | bytes 2696 | tf_op jit(solution)/shard_map/ppermute | solution.py:276
  28.6 0.8 collective-permute-done
  29.5 0.5 fusion.7
  30.0 0.6 iota_compare_fusion.2
  31.0 42.4 %all-to-all-done = bf16[32,2,128,128]{3,2,1,0:T(8,128)(2,1)S(1)} async-done(((bf16[32,2,128,128]{3,2,1,0:T(8,128)(2,1)}), bf16[32,2,128,128]{3,2,1,0:T(8,128)(2,1)S(1)}, u32[]{:S(2)}, u32[]{:S(2)}) %all-to-all-start) | async-done | bytes 2097184 | tf_op jit(solution)/shard_map/all_to_all | solution.py:285
  73.4 1.0 dynamic-slice_bitcast_fusion
  74.5 5.8 %collective-permute-start.2 = (bf16[16,2,128,128]{3,2,1,0:T(8,128)(2,1)}, bf16[16,2,128,128]{3,2,1,0:T(8,128)(2,1)S(1)}, u32[]{:S(2)}, u32[]{:S(2)}) collective-permute-start(bf16[16,2,128,128]{3,2,1,0:T(8,128)(2,1)} %dynamic-slice_bitcast_fusion), channel_id=1, source_target_pairs={{0,1},{1,0},{2,3},{3,2},{4,5},{5,4},{6,7},{7,6},{8,9},{9,8},{10,11... | collective-permute-start | bytes 3145736 | tf_op jit(solution)/shard_map/ppermute | solution.py:288
  80.2 0.7 iota_compare_fusion.1
  81.5 1.2 collective-permute-done.2.z_ref
  82.7 37.8 %attend.1 = (bf16[16,128,128]{2,1,0:T(8,128)(2,1)S(1)}, bf16[16,256,128]{2,1,0:T(8,128)(2,1)S(1)}, f32[16,256,128]{2,1,0:T(8,128)S(1)}) custom-call(s32[2]{0:T(128)S(1)} %copy-done, s32[16,13]{1,0:T(8,128)S(1)} %pad_add_fusion.2.tab_ref, bf16[2,16,2,128,128]{4,3,2,1,0:T(8,128)(2,1)S(1)} %bitcast.16, bf16[16,2,128,128]{3,2,1,0:T(8,128)(2,1)S(1)} %collective-permute-done.2.z_ref), custom_call_target="tpu_custom_call" | custom-call | tf_op jit(solution)/shard_map/attend/pallas_call | solution.py:160
  120.5 2.7 %collective-permute-start.3 = (bf16[16,256,128]{2,1,0:T(8,128)(2,1)S(1)}, bf16[16,256,128]{2,1,0:T(8,128)(2,1)S(1)}, u32[]{:S(2)}, u32[]{:S(2)}) collective-permute-start(bf16[16,256,128]{2,1,0:T(8,128)(2,1)S(1)} %get-tuple-element.12), channel_id=1, source_target_pairs={{0,1},{1,0},{2,3},{3,2},{4,5},{5,4},{6,7},{7,6},{8,9},{9,8},{10,11... | collective-permute-start | bytes 3145736 | tf_op jit(solution)/shard_map/ppermute | solution.py:291
  123.2 2.3 %collective-permute-done.3.got_ref = bf16[16,256,128]{2,1,0:T(8,128)(2,1)S(1)} collective-permute-done((bf16[16,256,128]{2,1,0:T(8,128)(2,1)S(1)}, bf16[16,256,128]{2,1,0:T(8,128)(2,1)S(1)}, u32[]{:S(2)}, u32[]{:S(2)}) %collective-permute-start.3) | collective-permute-done | bytes 1048608 | tf_op jit(solution)/shard_map/ppermute | solution.py:291
  125.5 0.7 join_partials.1
  126.2 45.6 %all_to_all.10 = bf16[32,192,128]{2,1,0:T(8,128)(2,1)S(1)} all-to-all(bf16[32,192,128]{2,1,0:T(8,128)(2,1)S(1)} %bitcast.17), channel_id=1, replica_groups=mesh['x'=4,'zh'=4,'zl'=2,'y'=8,'core'=2] {'zl','x','zh'}, dimensions={0} | all-to-all | bytes 3145728 | tf_op jit(solution)/shard_map/all_to_all | solution.py:294
  171.9 4.1 %collective-permute-start.4 = (bf16[16,192,128]{2,1,0:T(8,128)(2,1)S(1)}, bf16[16,192,128]{2,1,0:T(8,128)(2,1)S(1)}, u32[]{:S(2)}, u32[]{:S(2)}) collective-permute-start(bf16[16,192,128]{2,1,0:T(8,128)(2,1)S(1)} %dynamic-slice_bitcast_fusion.1), channel_id=1, source_target_pairs={{0,1},{1,0},{2,3},{3,2},{4,5},{5,4},{6,7},{7,6},{8,9},{9,8},{10,11... | collective-permute-start | bytes 2359304 | tf_op jit(solution)/shard_map/ppermute | solution.py:297
  176.0 1.9 %collective-permute-done.4.got_ref = bf16[16,192,128]{2,1,0:T(8,128)(2,1)S(1)} collective-permute-done((bf16[16,192,128]{2,1,0:T(8,128)(2,1)S(1)}, bf16[16,192,128]{2,1,0:T(8,128)(2,1)S(1)}, u32[]{:S(2)}, u32[]{:S(2)}) %collective-permute-start.4) | collective-permute-done | bytes 786464 | tf_op jit(solution)/shard_map/ppermute | solution.py:297
  177.9 0.9 copy-done.2
  178.8 4.4 %merge_heads.1 = (bf16[128,2048]{1,0:T(8,128)(2,1)}, bf16[128,2048]{1,0:T(8,128)(2,1)}, bf16[128,2048]{1,0:T(8,128)(2,1)}) custom-call(s32[2]{0:T(128)} %pad_add_fusion.4.sc_ref, bf16[2,16,192,128]{3,2,1,0:T(8,128)(2,1)} %bitcast.19, bf16[16,192,128]{2,1,0:T(8,128)(2,1)} %copy-done.2), custom_call_target="tpu_custom_call" | custom-call | tf_op jit(solution)/shard_map/merge_heads/pallas_call | solution.py:226
  (28 shorter events, 1.1 us)
Async XLA Ops:
  6.0 11.3 %collective-permute-start.1 = (bf16[16,2,128,128]{3,2,1,0:T(8,128)(2,1)}, bf16[16,2,128,128]{3,2,1,0:T(8,128)(2,1)S(1)}, u32[]{:S(2)}, u32[]{:S(2)}) collective-permute-start(bf16[16,2,128,128]{3,2,1,0:T(8,128)(2,1)} %get-tuple-element.9), channel_id=1, source_target_pairs={{0,1},{1,0},{2,3},{3,2},{4,5},{5,4},{6,7},{7,6},{8,9},{9,8},{10,11... | collective-permute-start | bytes 3145736 | tf_op jit(solution)/shard_map/ppermute | solution.py:282
  18.3 7.6 %copy-start.3 = (s32[16,6]{0,1:T(8,128)S(1)}, s32[16,6]{0,1:T(8,128)}, u32[]{:S(2)}) copy-start(s32[16,6]{0,1:T(8,128)} %param.12) | copy-start | bytes 1156
  18.3 7.7 %copy-start.4 = (s32[16,6]{0,1:T(8,128)S(1)}, s32[16,6]{0,1:T(8,128)}, u32[]{:S(2)}) copy-start(s32[16,6]{0,1:T(8,128)} %param.11) | copy-start | bytes 1156
  18.3 7.7 %copy-start.5 = (s32[16,2]{0,1:T(2,128)S(1)}, s32[16,2]{0,1:T(2,128)}, u32[]{:S(2)}) copy-start(s32[16,2]{0,1:T(2,128)} %param.13) | copy-start | bytes 388
  18.3 55.1 %all-to-all-start = ((bf16[32,2,128,128]{3,2,1,0:T(8,128)(2,1)}), bf16[32,2,128,128]{3,2,1,0:T(8,128)(2,1)S(1)}, u32[]{:S(2)}, u32[]{:S(2)}) async-start(bf16[32,2,128,128]{3,2,1,0:T(8,128)(2,1)} %bitcast.20), calls=%async_computation | async-start | bytes 4194304 | tf_op jit(solution)/shard_map/all_to_all | solution.py:285
  26.0 56.7 %copy-start = (s32[2]{0:T(128)S(1)}, s32[2]{0:T(128)}, u32[]{:S(2)}) copy-start(s32[2]{0:T(128)} %pad_add_fusion.4.sc_ref) | copy-start | bytes 28
  26.0 3.4 %collective-permute-start = (s32[16,14]{0,1:T(8,128)S(1)}, s32[16,14]{0,1:T(8,128)S(1)}, u32[]{:S(2)}, u32[]{:S(2)}) collective-permute-start(s32[16,14]{0,1:T(8,128)S(1)} %pad_add_fusion), channel_id=1, source_target_pairs={{0,1},{1,0},{2,3},{3,2},{4,5},{5,4},{6,7},{7,6},{8,9},{9,8},{10,11... | collective-permute-start | bytes 2696 | tf_op jit(solution)/shard_map/ppermute | solution.py:276
  74.5 8.2 %collective-permute-start.2 = (bf16[16,2,128,128]{3,2,1,0:T(8,128)(2,1)}, bf16[16,2,128,128]{3,2,1,0:T(8,128)(2,1)S(1)}, u32[]{:S(2)}, u32[]{:S(2)}) collective-permute-start(bf16[16,2,128,128]{3,2,1,0:T(8,128)(2,1)} %dynamic-slice_bitcast_fusion), channel_id=1, source_target_pairs={{0,1},{1,0},{2,3},{3,2},{4,5},{5,4},{6,7},{7,6},{8,9},{9,8},{10,11... | collective-permute-start | bytes 3145736 | tf_op jit(solution)/shard_map/ppermute | solution.py:288
  120.5 5.0 %collective-permute-start.3 = (bf16[16,256,128]{2,1,0:T(8,128)(2,1)S(1)}, bf16[16,256,128]{2,1,0:T(8,128)(2,1)S(1)}, u32[]{:S(2)}, u32[]{:S(2)}) collective-permute-start(bf16[16,256,128]{2,1,0:T(8,128)(2,1)S(1)} %get-tuple-element.12), channel_id=1, source_target_pairs={{0,1},{1,0},{2,3},{3,2},{4,5},{5,4},{6,7},{7,6},{8,9},{9,8},{10,11... | collective-permute-start | bytes 3145736 | tf_op jit(solution)/shard_map/ppermute | solution.py:291
  171.9 6.0 %copy-start.1 = (bf16[32,192,128]{2,1,0:T(8,128)(2,1)}, bf16[32,192,128]{2,1,0:T(8,128)(2,1)S(1)}, u32[]{:S(2)}) copy-start(bf16[32,192,128]{2,1,0:T(8,128)(2,1)S(1)} %all_to_all.10) | copy-start | bytes 4718596
  171.9 6.0 %collective-permute-start.4 = (bf16[16,192,128]{2,1,0:T(8,128)(2,1)S(1)}, bf16[16,192,128]{2,1,0:T(8,128)(2,1)S(1)}, u32[]{:S(2)}, u32[]{:S(2)}) collective-permute-start(bf16[16,192,128]{2,1,0:T(8,128)(2,1)S(1)} %dynamic-slice_bitcast_fusion.1), channel_id=1, source_target_pairs={{0,1},{1,0},{2,3},{3,2},{4,5},{5,4},{6,7},{7,6},{8,9},{9,8},{10,11... | collective-permute-start | bytes 2359304 | tf_op jit(solution)/shard_map/ppermute | solution.py:297
  177.9 0.9 copy-start.2

commit v2 on v1

v2 whole, which is shorter than its diff:
```python
import functools

import jax
import jax.numpy as jnp
from jax import lax
from jax.experimental import pallas as pl
from jax.experimental.pallas import tpu as pltpu
from jax.sharding import Mesh
from jax.sharding import PartitionSpec as P

HEADS = 16
HEAD_DIM = 128
BLK = 128
NBLOCKS = 32
HALF = NBLOCKS // 2
SLOTS = 12
TOGETHER = 4
SCALE = HEAD_DIM ** (-0.5)
ORDER = ("zl", "x", "zh")
SWAP = [(0, 1), (1, 0)]
NEG = -1e30
VMEM_SPEC = pl.BlockSpec(memory_space=pltpu.VMEM)
ANY_SPEC = pl.BlockSpec(memory_space=pl.ANY)
HBM_SPEC = pl.BlockSpec(memory_space=pltpu.HBM)
SMEM_SPEC = pl.BlockSpec(memory_space=pltpu.SMEM)


def head_cols(h):
    return pl.ds(h * HEAD_DIM, HEAD_DIM)


def take_pair(first, second, target, sems):
    copies = [
        pltpu.make_async_copy(source.at[:, head_cols(h)], target.at[h, i], sems.at[2 * h + i])
        for h in range(HEADS)
        for i, source in enumerate((first, second))
    ]
    for copy in copies:
        copy.start()
    for copy in copies:
        copy.wait()


def sent_kernel(sc_ref, q_ref, k_ref, v_ref, d_ref, sent_ref, sems):
    @pl.when(sc_ref[1] == 1)
    def _():
        take_pair(k_ref, v_ref, sent_ref, sems)

    @pl.when(sc_ref[1] == 0)
    def _():
        take_pair(q_ref, d_ref, sent_ref, sems)


def kept_kernel(sc_ref, q_ref, k_ref, v_ref, d_ref, kept_ref, sems):
    mine = kept_ref.at[sc_ref[0]]

    @pl.when(sc_ref[1] == 1)
    def _():
        take_pair(q_ref, d_ref, mine, sems)

    @pl.when(sc_ref[1] == 0)
    def _():
        take_pair(k_ref, v_ref, mine, sems)


def pair_call(kernel, lead, grant, name, scalars, q, k, v, d):
    return pl.pallas_call(
        kernel,
        in_specs=[SMEM_SPEC] + [HBM_SPEC] * 4,
        out_specs=VMEM_SPEC,
        out_shape=jax.ShapeDtypeStruct(lead + (HEADS, 2, BLK, HEAD_DIM), jnp.bfloat16),
        scratch_shapes=[pltpu.SemaphoreType.DMA((2 * HEADS,))],
        cost_estimate=pl.CostEstimate(flops=0, transcendentals=0, bytes_accessed=4 * 2**20),
        compiler_params=pltpu.CompilerParams(vmem_limit_bytes=grant * 2**20),
        name=name,
    )(scalars, q, k, v, d)


def attend_kernel(
    sc_ref, tab_ref, y_ref, z_ref, dq_ref, send_ref, loc_ref, keys, values, dk_acc, dv_acc
):
    core = sc_ref[0]

    @pl.loop(0, HALF, unroll=4)
    def _(m):
        for t, k_tile, v_tile in (
            (m, z_ref[m, 0], z_ref[m, 1]),
            (HALF + m, y_ref[1 - core, m, 0], y_ref[1 - core, m, 1]),
        ):
            keys[t] = k_tile
            values[t] = v_tile
            dk_acc[t] = jnp.zeros((BLK, HEAD_DIM), jnp.float32)
            dv_acc[t] = jnp.zeros((BLK, HEAD_DIM), jnp.float32)

    @pl.loop(0, HALF // TOGETHER)
    def _(step):
        rows = [tab_ref[TOGETHER * step + r, SLOTS + 1] for r in range(TOGETHER)]
        counts = [tab_ref[m, SLOTS] for m in rows]
        pairs = (functools.reduce(jnp.maximum, counts) + 1) // 2

        for groups in range(1, SLOTS // 2 + 1):

            @pl.when(pairs == groups)
            def _(groups=groups):
                slots = range(2 * groups)
                scored = []
                for m, count in zip(rows, counts):
                    q = y_ref[core, m, 0]
                    d = y_ref[core, m, 1]
                    places = [tab_ref[m, a] for a in slots]
                    k_rows = jnp.concatenate([keys[t] for t in places], axis=0)
                    v_rows = jnp.concatenate([values[t] for t in places], axis=0)
                    s = jnp.dot(k_rows, q.T, preferred_element_type=jnp.float32)
                    g = jnp.dot(v_rows, d.T, preferred_element_type=jnp.float32)
                    s = jnp.concatenate(
                        [
                            s[a * BLK : (a + 1) * BLK] + jnp.where(a < count, 0.0, NEG)
                            for a in slots
                        ],
                        axis=0,
                    )
                    scored.append((m, q, d, places, k_rows, s, g))
                formed = []
                for m, q, d, places, k_rows, s, g in scored:
                    top = jnp.max(s, axis=0, keepdims=True)
                    e = jnp.exp((s - top) * SCALE)
                    inverse = 1.0 / jnp.sum(e, axis=0, keepdims=True)
                    delta = jnp.sum(e * g, axis=0, keepdims=True) * inverse
                    p = e * inverse
                    w = p.astype(jnp.bfloat16)
                    ds = (p * (g - delta)).astype(jnp.bfloat16)
                    formed.append((m, q, d, places, k_rows, w, ds))
                for m, q, d, places, k_rows, w, ds in formed:
                    for_keys = jnp.dot(ds, q, preferred_element_type=jnp.float32)
                    for_values = jnp.dot(w, d, preferred_element_type=jnp.float32)
                    for a in slots:
                        part = slice(a * BLK, (a + 1) * BLK)
                        dk_acc[places[a]] += for_keys[part]
                        dv_acc[places[a]] += for_values[part]
                    dq = lax.dot_general(
                        ds, k_rows, (((0,), (0,)), ((), ())), preferred_element_type=jnp.float32
                    )
                    dq_ref[m] = (dq * SCALE).astype(jnp.bfloat16)

    hb = BLK // 2

    @pl.loop(0, HALF, unroll=4)
    def _(m):
        far = HALF + m
        send_ref[m, :BLK] = (dk_acc[m] * SCALE).astype(jnp.bfloat16)
        send_ref[m, BLK : BLK + hb] = dv_acc[m, hb:].astype(jnp.bfloat16)
        send_ref[m, BLK + hb :] = dv_acc[far, :hb].astype(jnp.bfloat16)
        loc_ref[m, :BLK] = dk_acc[far] * SCALE
        loc_ref[m, BLK : BLK + hb] = dv_acc[far, hb:]
        loc_ref[m, BLK + hb :] = dv_acc[m, :hb]


def attend_call(scalars, table, y, z):
    return pl.pallas_call(
        attend_kernel,
        in_specs=[SMEM_SPEC, SMEM_SPEC, VMEM_SPEC, VMEM_SPEC],
        out_specs=[VMEM_SPEC, VMEM_SPEC, VMEM_SPEC],
        out_shape=[
            jax.ShapeDtypeStruct((HALF, BLK, HEAD_DIM), jnp.bfloat16),
            jax.ShapeDtypeStruct((HALF, 2 * BLK, HEAD_DIM), jnp.bfloat16),
            jax.ShapeDtypeStruct((HALF, 2 * BLK, HEAD_DIM), jnp.float32),
        ],
        scratch_shapes=[
            pltpu.VMEM((NBLOCKS, BLK, HEAD_DIM), jnp.bfloat16),
            pltpu.VMEM((NBLOCKS, BLK, HEAD_DIM), jnp.bfloat16),
            pltpu.VMEM((NBLOCKS, BLK, HEAD_DIM), jnp.float32),
            pltpu.VMEM((NBLOCKS, BLK, HEAD_DIM), jnp.float32),
        ],
        compiler_params=pltpu.CompilerParams(vmem_limit_bytes=24 * 2**20),
        name="attend",
    )(scalars, table, y, z)


def join_kernel(sc_ref, dq_ref, loc_ref, got_ref, out_ref):
    core = sc_ref[0]
    hb = BLK // 2
    summed = (loc_ref[...] + got_ref[...].astype(jnp.float32)).astype(jnp.bfloat16)
    out_ref[core, :, :BLK] = dq_ref[...]
    out_ref[core, :, BLK:] = summed[:, BLK + hb :]
    out_ref[1 - core] = summed[:, : BLK + hb]


def join_call(scalars, dq, loc, got):
    return pl.pallas_call(
        join_kernel,
        in_specs=[SMEM_SPEC, VMEM_SPEC, VMEM_SPEC, VMEM_SPEC],
        out_specs=VMEM_SPEC,
        out_shape=jax.ShapeDtypeStruct((2, HALF, BLK + BLK // 2, HEAD_DIM), jnp.bfloat16),
        compiler_params=pltpu.CompilerParams(vmem_limit_bytes=10 * 2**20),
        name="join_partials",
    )(scalars, dq, loc, got)


def put_pair(source, wide, narrow, half, sems):
    hb = BLK // 2
    copies = []
    for h in range(HEADS):
        copies.append(
            pltpu.make_async_copy(
                source.at[h, pl.ds(0, BLK)], wide.at[:, head_cols(h)], sems.at[2 * h]
            )
        )
        copies.append(
            pltpu.make_async_copy(
                source.at[h, pl.ds(BLK, hb)],
                narrow.at[pl.ds(half * hb, hb), head_cols(h)],
                sems.at[2 * h + 1],
            )
        )
    for copy in copies:
        copy.start()
    for copy in copies:
        copy.wait()


def own_kernel(sc_ref, own_ref, dq_ref, dk_ref, dv_ref, sems):
    mine = own_ref.at[sc_ref[0]]

    @pl.when(sc_ref[1] == 1)
    def _():
        put_pair(mine, dq_ref, dv_ref, 0, sems)

    @pl.when(sc_ref[1] == 0)
    def _():
        put_pair(mine, dk_ref, dv_ref, 1, sems)


def other_kernel(sc_ref, got_ref, dq_in, dk_in, dv_in, dq_ref, dk_ref, dv_ref, sems):
    del dq_in, dk_in, dv_in

    @pl.when(sc_ref[1] == 1)
    def _():
        put_pair(got_ref, dk_ref, dv_ref, 1, sems)

    @pl.when(sc_ref[1] == 0)
    def _():
        put_pair(got_ref, dq_ref, dv_ref, 0, sems)


def place_call(kernel, name, scalars, part, so_far):
    shape = jax.ShapeDtypeStruct((BLK, HEADS * HEAD_DIM), jnp.bfloat16)
    return pl.pallas_call(
        kernel,
        in_specs=[SMEM_SPEC, ANY_SPEC] + [HBM_SPEC] * len(so_far),
        out_specs=[HBM_SPEC] * 3,
        out_shape=[shape] * 3,
        input_output_aliases={2 + i: i for i in range(len(so_far))},
        scratch_shapes=[pltpu.SemaphoreType.DMA((2 * HEADS,))],
        cost_estimate=pl.CostEstimate(flops=0, transcendentals=0, bytes_accessed=4 * 2**20),
        compiler_params=pltpu.CompilerParams(vmem_limit_bytes=4 * 2**20),
        name=name,
    )(scalars, part, *so_far)


def block_table(vert, slash, count, core):
    chosen = core + 2 * jnp.arange(HALF, dtype=jnp.int32)
    vert_index = jnp.broadcast_to(vert[None, :], (HALF, vert.shape[0]))
    vert_valid = jnp.broadcast_to(
        (jnp.arange(vert.shape[0], dtype=jnp.int32) < count[0])[None, :], vert_index.shape
    )
    slash_index = chosen[:, None] - slash[None, :]
    inside = (slash_index >= 0) & (slash_index < NBLOCKS)
    repeated = jnp.any(
        (vert_index[:, :, None] == slash_index[:, None, :]) & vert_valid[:, :, None], axis=1
    )
    slash_valid = (
        (jnp.arange(slash.shape[0], dtype=jnp.int32) < count[1])[None, :]
        & inside
        & jnp.logical_not(repeated)
    )
    index = jnp.concatenate([vert_index, slash_index], axis=1)
    valid = jnp.concatenate([vert_valid, slash_valid], axis=1)
    place = ((index & 1) ^ core) * HALF + (index >> 1)
    rank = jnp.cumsum(valid.astype(jnp.int32), axis=1) - 1
    lanes = jnp.arange(SLOTS, dtype=jnp.int32)
    hit = valid[:, :, None] & (rank[:, :, None] == lanes[None, None, :])
    packed = jnp.sum(jnp.where(hit, place[:, :, None], 0), axis=1)
    total = jnp.sum(valid.astype(jnp.int32), axis=1, keepdims=True)
    m = jnp.arange(HALF, dtype=jnp.int32)
    ahead = (total[None, :, 0] > total) | ((total[None, :, 0] == total) & (m[None, :] < m[:, None]))
    rank_of = jnp.sum(ahead.astype(jnp.int32), axis=1)
    order = jnp.sum(jnp.where(rank_of[None, :] == m[:, None], m[None, :], 0), axis=1, keepdims=True)
    return jnp.concatenate([packed, total, order], axis=1)


def body(queries, key_rows, value_rows, out_grad, vertical, slash_offsets, counts):
    core = lax.axis_index("core")
    parity = lax.axis_index("zl")
    head = lax.axis_index("x") * lax.axis_size("zh") + lax.axis_index("zh")
    scalars = jnp.stack([core, (core == parity).astype(jnp.int32)]).astype(jnp.int32)

    tables = jnp.concatenate([vertical, slash_offsets, counts], axis=1)
    other_tables = lax.ppermute(tables, "core", SWAP)
    row = jnp.where(core == parity, tables[head], other_tables[head])
    nv, ns = vertical.shape[1], slash_offsets.shape[1]
    table = block_table(row[:nv], row[nv : nv + ns], row[nv + ns :], core)

    rows = tuple(
        pltpu.with_memory_space_constraint(x, pltpu.HBM)
        for x in (queries, key_rows, value_rows, out_grad)
    )
    sent = pair_call(sent_kernel, (), 4, "take_sent", scalars, *rows)
    got = lax.ppermute(sent, "core", SWAP)
    kept = pair_call(kept_kernel, (2,), 60, "take_kept", scalars, *rows)
    kept = lax.dynamic_update_slice(kept, got[None], (1 - core, 0, 0, 0, 0))
    spread = kept.reshape(NBLOCKS, 2, BLK, HEAD_DIM)
    arrived = lax.all_to_all(spread, ORDER, split_axis=0, concat_axis=0, tiled=True)
    arrived = arrived.reshape(2, HALF, 2, BLK, HEAD_DIM)
    far_keys = lax.dynamic_index_in_dim(arrived, 1 - core, 0, keepdims=False)
    near_keys = lax.ppermute(far_keys, "core", SWAP)

    dq, partial, local = attend_call(scalars, table, arrived, near_keys)
    got_partial = lax.ppermute(partial, "core", SWAP)
    outgoing = join_call(scalars, dq, local, got_partial)
    outgoing = outgoing.reshape(NBLOCKS, BLK + BLK // 2, HEAD_DIM)
    returned = lax.all_to_all(outgoing, ORDER, split_axis=0, concat_axis=0, tiled=True)
    returned = returned.reshape(2, HALF, BLK + BLK // 2, HEAD_DIM)
    for_other = lax.dynamic_index_in_dim(returned, 1 - core, 0, keepdims=False)
    from_other = lax.ppermute(for_other, "core", SWAP)
    so_far = place_call(own_kernel, "place_own", scalars, returned, ())
    return tuple(place_call(other_kernel, "place_other", scalars, from_other, so_far))


def solution(mesh):
    devices = mesh.devices
    fine = Mesh(devices.reshape(4, 4, 2, 8, 2), ("x", "zh", "zl", "y", "core"))
    rows = P(("y", "core", "x", "zh", "zl"), None)
    lists = P(("y", "core"), None)
    return jax.shard_map(
        body,
        mesh=fine,
        in_specs=(rows, rows, rows, rows, lists, lists, lists),
        out_specs=(rows, rows, rows),
        check_vma=False,
    )
```

time: 184 us -> 152 us (0.83)
  Pallas kernels: 47.6 us -> 20.2 us
  waiting for transfers between devices: 51 us -> 48 us
  starting transfers between devices: 31.6 us -> 29.3 us
  blocking collectives: 45.6 us -> 47.7 us
    pallas_call x1, Pallas kernels: 37.8 us -> 10.5 us  [attend_call(): pl.pallas_call(attend_kernel, in_specs=[SMEM_SPEC, SMEM_SPEC, VMEM_SPEC,...]
    ppermute x1, waiting for transfers between devices: 2.47 us -> 0.01 us  [body(): got = lax.ppermute(sent, 'core', SWAP)]
    all_to_all x1, blocking collectives: 45.6 us -> 47.7 us  [body(): lax.all_to_all(outgoing, ORDER, split_axis=0, concat_axis=0, tiled=True)]
    pallas_call x2 -> x4, Pallas kernels: 9.06 us -> 8.92 us  [the longest x2 5.53 us: pair_call(): pl.pallas_call(kernel, in_specs=[SMEM_SPEC] + [HBM_SPEC] * 4, out_specs=V...]
  transfers between devices with their start and end apart: 6 -> 6, of which waited for: 6 -> 5; matrix products, arithmetic and copies ran while one was open for 2% -> 2% of each run, Pallas kernels for 0% -> 3%
where the time goes in v2:
time: 152 us
  waiting for transfers between devices  48 us (32%)
  blocking collectives  47.7 us (31%)
  starting transfers between devices  29.3 us (19%)
  Pallas kernels  20.2 us (13%)
  local copies, waits for them, and re-layouts  3.05 us (2%)
  other arithmetic  2.41 us (2%)
    all_to_all x1, blocking collectives, body(): lax.all_to_all(outgoing, ORDER, split_axis=0, concat_axis=0, tiled=True)  47.7 us
    all_to_all x1, waiting for transfers between devices, body(): lax.all_to_all(spread, ORDER, split_axis=0, concat_axis=0, tiled=True)  42.9 us
    pallas_call x1, Pallas kernels, attend_call(): pl.pallas_call(attend_kernel, in_specs=[SMEM_SPEC, SMEM_SPEC, VMEM_SPEC,...  10.5 us
    ppermute x1, starting transfers between devices, body(): got = lax.ppermute(sent, 'core', SWAP)  8.78 us
    all_to_all x1, starting transfers between devices, body(): lax.all_to_all(spread, ORDER, split_axis=0, concat_axis=0, tiled=True)  7.64 us
    pallas_call x2, Pallas kernels, pair_call(): pl.pallas_call(kernel, in_specs=[SMEM_SPEC] + [HBM_SPEC] * 4, out_specs=V...  5.53 us
    ppermute x1, starting transfers between devices, body(): near_keys = lax.ppermute(far_keys, 'core', SWAP)  4.65 us
    ppermute x1, starting transfers between devices, body(): from_other = lax.ppermute(for_other, 'core', SWAP)  4.08 us
  transfers between devices with their start and end apart: 6, of which 5 were waited for; matrix products, arithmetic and copies ran while one was open for 2% of the time, Pallas kernels for 3%

profile of v2, /device:TPU:1, one launch (start us, length us, event | category | flops | bytes accessed | tf_op | source)
XLA Modules:
  0.0 151.6 jit_solution(9964207114669138326)
XLA Ops:
  0.7 2.0 %take_sent.1 = bf16[16,2,128,128]{3,2,1,0:T(8,128)(2,1)S(1)} custom-call(s32[2]{0:T(128)S(1)} %pad_add_fusion.4.sc_ref, bf16[128,2048]{1,0:T(8,128)(2,1)} %q_ref.3, bf16[128,2048]{1,0:T(8,128)(2,1)} %k_ref.3, bf16[128,2048]{1,0:T(8,128)(2,1)} %v_ref.3, bf16[128,2048]{1,0:T(8,128)(2,1)} %d_ref.3), custom_call_target="tpu_custom_call" | custom-call | bytes 4194304 | tf_op jit(solution)/shard_map/take_sent/pallas_call | solution.py:67
  2.8 8.8 %collective-permute-start.1 = (bf16[16,2,128,128]{3,2,1,0:T(8,128)(2,1)S(1)}, bf16[16,2,128,128]{3,2,1,0:T(8,128)(2,1)S(1)}, u32[]{:S(2)}, u32[]{:S(2)}) collective-permute-start(bf16[16,2,128,128]{3,2,1,0:T(8,128)(2,1)S(1)} %take_sent.1), channel_id=1, source_target_pairs={{0,1},{1,0},{2,3},{3,2},{4,5},{5,4},{6,7},{7,6},{8,9},{9,8},{10,11... | collective-permute-start | bytes 3145736 | tf_op jit(solution)/shard_map/ppermute | solution.py:308
  11.5 3.5 %take_kept.1 = bf16[2,16,2,128,128]{4,3,2,1,0:T(8,128)(2,1)} custom-call(s32[2]{0:T(128)} %copy-done, bf16[128,2048]{1,0:T(8,128)(2,1)} %q_ref.3, bf16[128,2048]{1,0:T(8,128)(2,1)} %k_ref.3, bf16[128,2048]{1,0:T(8,128)(2,1)} %v_ref.3, bf16[128,2048]{1,0:T(8,128)(2,1)} %d_ref.3), custom_call_target="tpu_custom_call" | custom-call | bytes 4194304 | tf_op jit(solution)/shard_map/take_kept/pallas_call | solution.py:67
  15.1 1.1 bitcast_dynamic-update-slice_fusion
  16.1 7.6 %all-to-all-start = ((bf16[32,2,128,128]{3,2,1,0:T(8,128)(2,1)}), bf16[32,2,128,128]{3,2,1,0:T(8,128)(2,1)S(1)}, u32[]{:S(2)}, u32[]{:S(2)}) async-start(bf16[32,2,128,128]{3,2,1,0:T(8,128)(2,1)} %bitcast.21), calls=%async_computation | async-start | bytes 4194304 | tf_op jit(solution)/shard_map/all_to_all | solution.py:312
  23.9 2.3 %collective-permute-start = (s32[16,14]{0,1:T(8,128)S(1)}, s32[16,14]{0,1:T(8,128)S(1)}, u32[]{:S(2)}, u32[]{:S(2)}) collective-permute-start(s32[16,14]{0,1:T(8,128)S(1)} %pad_add_fusion), channel_id=1, source_target_pairs={{0,1},{1,0},{2,3},{3,2},{4,5},{5,4},{6,7},{7,6},{8,9},{9,8},{10,11... | collective-permute-start | bytes 2696 | tf_op jit(solution)/shard_map/ppermute | solution.py:298
  26.1 0.8 collective-permute-done
  27.0 0.5 fusion.9
  27.5 0.6 iota_compare_fusion.3
  28.2 0.6 iota_compare_fusion.4
  29.1 42.9 %all-to-all-done = bf16[32,2,128,128]{3,2,1,0:T(8,128)(2,1)S(1)} async-done(((bf16[32,2,128,128]{3,2,1,0:T(8,128)(2,1)}), bf16[32,2,128,128]{3,2,1,0:T(8,128)(2,1)S(1)}, u32[]{:S(2)}, u32[]{:S(2)}) %all-to-all-start) | async-done | bytes 2097184 | tf_op jit(solution)/shard_map/all_to_all | solution.py:312
  72.0 1.1 dynamic-slice_bitcast_fusion
  73.1 4.6 %collective-permute-start.2 = (bf16[16,2,128,128]{3,2,1,0:T(8,128)(2,1)}, bf16[16,2,128,128]{3,2,1,0:T(8,128)(2,1)S(1)}, u32[]{:S(2)}, u32[]{:S(2)}) collective-permute-start(bf16[16,2,128,128]{3,2,1,0:T(8,128)(2,1)} %dynamic-slice_bitcast_fusion), channel_id=1, source_target_pairs={{0,1},{1,0},{2,3},{3,2},{4,5},{5,4},{6,7},{7,6},{8,9},{9,8},{10,11... | collective-permute-start | bytes 3145736 | tf_op jit(solution)/shard_map/ppermute | solution.py:315
  78.0 0.2 convert_reduce_fusion
  78.8 1.5 collective-permute-done.2.z_ref
  80.2 10.5 %attend.1 = (bf16[16,128,128]{2,1,0:T(8,128)(2,1)S(1)}, bf16[16,256,128]{2,1,0:T(8,128)(2,1)S(1)}, f32[16,256,128]{2,1,0:T(8,128)S(1)}) custom-call(s32[2]{0:T(128)S(1)} %copy-done.1, s32[16,14]{1,0:T(8,128)S(1)} %pad_add_fusion.2.tab_ref, bf16[2,16,2,128,128]{4,3,2,1,0:T(8,128)(2,1)S(1)} %bitcast.17, bf16[16,2,128,128]{3,2,1,0:T(8,128)(2,1)S(1)} %collective-permute-done.2.z_ref), custom_call_target="tpu_custom_call" | custom-call | tf_op jit(solution)/shard_map/attend/pallas_call | solution.py:159
  90.8 1.9 %collective-permute-start.3 = (bf16[16,256,128]{2,1,0:T(8,128)(2,1)S(1)}, bf16[16,256,128]{2,1,0:T(8,128)(2,1)S(1)}, u32[]{:S(2)}, u32[]{:S(2)}) collective-permute-start(bf16[16,256,128]{2,1,0:T(8,128)(2,1)S(1)} %get-tuple-element.11), channel_id=1, source_target_pairs={{0,1},{1,0},{2,3},{3,2},{4,5},{5,4},{6,7},{7,6},{8,9},{9,8},{10,11... | collective-permute-start | bytes 3145736 | tf_op jit(solution)/shard_map/ppermute | solution.py:318
  92.7 2.6 %collective-permute-done.3.got_ref = bf16[16,256,128]{2,1,0:T(8,128)(2,1)S(1)} collective-permute-done((bf16[16,256,128]{2,1,0:T(8,128)(2,1)S(1)}, bf16[16,256,128]{2,1,0:T(8,128)(2,1)S(1)}, u32[]{:S(2)}, u32[]{:S(2)}) %collective-permute-start.3) | collective-permute-done | bytes 1048608 | tf_op jit(solution)/shard_map/ppermute | solution.py:318
  95.3 0.7 join_partials.1
  96.1 47.7 %all_to_all.10 = bf16[32,192,128]{2,1,0:T(8,128)(2,1)S(1)} all-to-all(bf16[32,192,128]{2,1,0:T(8,128)(2,1)S(1)} %bitcast.20), channel_id=1, replica_groups=mesh['x'=4,'zh'=4,'zl'=2,'y'=8,'core'=2] {'zl','x','zh'}, dimensions={0} | all-to-all | bytes 3145728 | tf_op jit(solution)/shard_map/all_to_all | solution.py:321
  143.9 4.1 %collective-permute-start.4 = (bf16[16,192,128]{2,1,0:T(8,128)(2,1)S(1)}, bf16[16,192,128]{2,1,0:T(8,128)(2,1)S(1)}, u32[]{:S(2)}, u32[]{:S(2)}) collective-permute-start(bf16[16,192,128]{2,1,0:T(8,128)(2,1)S(1)} %dynamic-slice_bitcast_fusion.1), channel_id=1, source_target_pairs={{0,1},{1,0},{2,3},{3,2},{4,5},{5,4},{6,7},{7,6},{8,9},{9,8},{10,11... | collective-permute-start | bytes 2359304 | tf_op jit(solution)/shard_map/ppermute | solution.py:324
  148.0 1.7 %place_own.1 = (bf16[128,2048]{1,0:T(8,128)(2,1)}, bf16[128,2048]{1,0:T(8,128)(2,1)}, bf16[128,2048]{1,0:T(8,128)(2,1)}) custom-call(s32[2]{0:T(128)S(1)} %copy-done.1, bf16[2,16,192,128]{3,2,1,0:T(8,128)(2,1)S(1)} %bitcast.19), custom_call_target="tpu_custom_call" | custom-call | bytes 4194304 | tf_op jit(solution)/shard_map/place_own/pallas_call | solution.py:247
  149.7 0.2 collective-permute-done.4.got_ref
  149.9 1.7 %place_other.1 = (bf16[128,2048]{1,0:T(8,128)(2,1)}, bf16[128,2048]{1,0:T(8,128)(2,1)}, bf16[128,2048]{1,0:T(8,128)(2,1)}) custom-call(s32[2]{0:T(128)S(1)} %copy-done.1, bf16[16,192,128]{2,1,0:T(8,128)(2,1)S(1)} %collective-permute-done.4.got_ref, ...), custom_call_target="tpu_custom_call", output_to_operand_aliasing={{0}: (2, {}), {1}: (3, {}), {2}: (4, {})} | custom-call | bytes 4194304 | tf_op jit(solution)/shard_map/place_other/pallas_call | solution.py:247
  (31 shorter events, 1.4 us)
Async XLA Ops:
  0.7 10.8 %copy-start = (s32[2]{0:T(128)}, s32[2]{0:T(128)S(1)}, u32[]{:S(2)}) copy-start(s32[2]{0:T(128)S(1)} %pad_add_fusion.4.sc_ref) | copy-start | bytes 28
  2.8 12.3 %collective-permute-start.1 = (bf16[16,2,128,128]{3,2,1,0:T(8,128)(2,1)S(1)}, bf16[16,2,128,128]{3,2,1,0:T(8,128)(2,1)S(1)}, u32[]{:S(2)}, u32[]{:S(2)}) collective-permute-start(bf16[16,2,128,128]{3,2,1,0:T(8,128)(2,1)S(1)} %take_sent.1), channel_id=1, source_target_pairs={{0,1},{1,0},{2,3},{3,2},{4,5},{5,4},{6,7},{7,6},{8,9},{9,8},{10,11... | collective-permute-start | bytes 3145736 | tf_op jit(solution)/shard_map/ppermute | solution.py:308
  16.1 7.7 %copy-start.2 = (s32[16,6]{0,1:T(8,128)S(1)}, s32[16,6]{0,1:T(8,128)}, u32[]{:S(2)}) copy-start(s32[16,6]{0,1:T(8,128)} %param.12) | copy-start | bytes 1156
  16.1 7.7 %copy-start.3 = (s32[16,6]{0,1:T(8,128)S(1)}, s32[16,6]{0,1:T(8,128)}, u32[]{:S(2)}) copy-start(s32[16,6]{0,1:T(8,128)} %param.11) | copy-start | bytes 1156
  16.1 7.7 %copy-start.4 = (s32[16,2]{0,1:T(2,128)S(1)}, s32[16,2]{0,1:T(2,128)}, u32[]{:S(2)}) copy-start(s32[16,2]{0,1:T(2,128)} %param.13) | copy-start | bytes 388
  16.1 55.9 %all-to-all-start = ((bf16[32,2,128,128]{3,2,1,0:T(8,128)(2,1)}), bf16[32,2,128,128]{3,2,1,0:T(8,128)(2,1)S(1)}, u32[]{:S(2)}, u32[]{:S(2)}) async-start(bf16[32,2,128,128]{3,2,1,0:T(8,128)(2,1)} %bitcast.21), calls=%async_computation | async-start | bytes 4194304 | tf_op jit(solution)/shard_map/all_to_all | solution.py:312
  23.8 56.4 %copy-start.1 = (s32[2]{0:T(128)S(1)}, s32[2]{0:T(128)}, u32[]{:S(2)}) copy-start(s32[2]{0:T(128)} %copy-done) | copy-start | bytes 28
  23.9 3.1 %collective-permute-start = (s32[16,14]{0,1:T(8,128)S(1)}, s32[16,14]{0,1:T(8,128)S(1)}, u32[]{:S(2)}, u32[]{:S(2)}) collective-permute-start(s32[16,14]{0,1:T(8,128)S(1)} %pad_add_fusion), channel_id=1, source_target_pairs={{0,1},{1,0},{2,3},{3,2},{4,5},{5,4},{6,7},{7,6},{8,9},{9,8},{10,11... | collective-permute-start | bytes 2696 | tf_op jit(solution)/shard_map/ppermute | solution.py:298
  73.1 7.1 %collective-permute-start.2 = (bf16[16,2,128,128]{3,2,1,0:T(8,128)(2,1)}, bf16[16,2,128,128]{3,2,1,0:T(8,128)(2,1)S(1)}, u32[]{:S(2)}, u32[]{:S(2)}) collective-permute-start(bf16[16,2,128,128]{3,2,1,0:T(8,128)(2,1)} %dynamic-slice_bitcast_fusion), channel_id=1, source_target_pairs={{0,1},{1,0},{2,3},{3,2},{4,5},{5,4},{6,7},{7,6},{8,9},{9,8},{10,11... | collective-permute-start | bytes 3145736 | tf_op jit(solution)/shard_map/ppermute | solution.py:315
  90.8 4.6 %collective-permute-start.3 = (bf16[16,256,128]{2,1,0:T(8,128)(2,1)S(1)}, bf16[16,256,128]{2,1,0:T(8,128)(2,1)S(1)}, u32[]{:S(2)}, u32[]{:S(2)}) collective-permute-start(bf16[16,256,128]{2,1,0:T(8,128)(2,1)S(1)} %get-tuple-element.11), channel_id=1, source_target_pairs={{0,1},{1,0},{2,3},{3,2},{4,5},{5,4},{6,7},{7,6},{8,9},{9,8},{10,11... | collective-permute-start | bytes 3145736 | tf_op jit(solution)/shard_map/ppermute | solution.py:318
  143.9 6.0 %collective-permute-start.4 = (bf16[16,192,128]{2,1,0:T(8,128)(2,1)S(1)}, bf16[16,192,128]{2,1,0:T(8,128)(2,1)S(1)}, u32[]{:S(2)}, u32[]{:S(2)}) collective-permute-start(bf16[16,192,128]{2,1,0:T(8,128)(2,1)S(1)} %dynamic-slice_bitcast_fusion.1), channel_id=1, source_target_pairs={{0,1},{1,0},{2,3},{3,2},{4,5},{5,4},{6,7},{7,6},{8,9},{9,8},{10,11... | collective-permute-start | bytes 2359304 | tf_op jit(solution)/shard_map/ppermute | solution.py:324

commit v3 on v2

--- a/solution.py
+++ b/solution.py
@@ -25,53 +25,63 @@
 SMEM_SPEC = pl.BlockSpec(memory_space=pltpu.SMEM)
 
 
-def head_cols(h):
-    return pl.ds(h * HEAD_DIM, HEAD_DIM)
-
-
-def take_pair(first, second, target, sems):
+CHUNK = 32
+
+
+def take_pair(first, second, target, rows_buf, sems):
+    parts = [
+        (i, r, source)
+        for r in range(0, BLK, CHUNK)
+        for i, source in enumerate((first, second))
+    ]
     copies = [
-        pltpu.make_async_copy(source.at[:, head_cols(h)], target.at[h, i], sems.at[2 * h + i])
-        for h in range(HEADS)
-        for i, source in enumerate((first, second))
+        pltpu.make_async_copy(
+            source.at[pl.ds(r, CHUNK)], rows_buf.at[i, pl.ds(r, CHUNK)], sems.at[n]
+        )
+        for n, (i, r, source) in enumerate(parts)
     ]
     for copy in copies:
         copy.start()
-    for copy in copies:
+    for copy, (i, r, _) in zip(copies, parts):
         copy.wait()
-
-
-def sent_kernel(sc_ref, q_ref, k_ref, v_ref, d_ref, sent_ref, sems):
+        for h in range(HEADS):
+            target[h, i, r : r + CHUNK] = rows_buf[
+                i, r : r + CHUNK, h * HEAD_DIM : (h + 1) * HEAD_DIM
+            ]
+
+
+def sent_kernel(sc_ref, q_ref, k_ref, v_ref, d_ref, sent_ref, rows_buf, sems):
     @pl.when(sc_ref[1] == 1)
     def _():
-        take_pair(k_ref, v_ref, sent_ref, sems)
+        take_pair(k_ref, v_ref, sent_ref, rows_buf, sems)
 
     @pl.when(sc_ref[1] == 0)
     def _():
-        take_pair(q_ref, d_ref, sent_ref, sems)
-
-
-def kept_kernel(sc_ref, q_ref, k_ref, v_ref, d_ref, kept_ref, sems):
-    mine = kept_ref.at[sc_ref[0]]
-
+        take_pair(q_ref, d_ref, sent_ref, rows_buf, sems)
+
+
+def kept_kernel(sc_ref, q_ref, k_ref, v_ref, d_ref, kept_ref, rows_buf, sems):
     @pl.when(sc_ref[1] == 1)
     def _():
-        take_pair(q_ref, d_ref, mine, sems)
+        take_pair(q_ref, d_ref, kept_ref, rows_buf, sems)
 
     @pl.when(sc_ref[1] == 0)
     def _():
-        take_pair(k_ref, v_ref, mine, sems)
-
-
-def pair_call(kernel, lead, grant, name, scalars, q, k, v, d):
+        take_pair(k_ref, v_ref, kept_ref, rows_buf, sems)
+
+
+def pair_call(kernel, name, scalars, q, k, v, d):
     return pl.pallas_call(
         kernel,
         in_specs=[SMEM_SPEC] + [HBM_SPEC] * 4,
         out_specs=VMEM_SPEC,
-        out_shape=jax.ShapeDtypeStruct(lead + (HEADS, 2, BLK, HEAD_DIM), jnp.bfloat16),
-        scratch_shapes=[pltpu.SemaphoreType.DMA((2 * HEADS,))],
+        out_shape=jax.ShapeDtypeStruct((HEADS, 2, BLK, HEAD_DIM), jnp.bfloat16),
+        scratch_shapes=[
+            pltpu.VMEM((2, BLK, HEADS * HEAD_DIM), jnp.bfloat16),
+            pltpu.SemaphoreType.DMA((2 * BLK // CHUNK,)),
+        ],
         cost_estimate=pl.CostEstimate(flops=0, transcendentals=0, bytes_accessed=4 * 2**20),
-        compiler_params=pltpu.CompilerParams(vmem_limit_bytes=grant * 2**20),
+        compiler_params=pltpu.CompilerParams(vmem_limit_bytes=4 * 2**20),
         name=name,
     )(scalars, q, k, v, d)
 
@@ -196,61 +206,66 @@
     )(scalars, dq, loc, got)
 
 
-def put_pair(source, wide, narrow, half, sems):
+def put_pair(source, wide, narrow, half, wide_buf, narrow_buf, sems):
     hb = BLK // 2
     copies = []
-    for h in range(HEADS):
-        copies.append(
-            pltpu.make_async_copy(
-                source.at[h, pl.ds(0, BLK)], wide.at[:, head_cols(h)], sems.at[2 * h]
-            )
+
+    def fill(buf, target, first_row, buf_row, target_row, n):
+        for h in range(HEADS):
+            buf[buf_row : buf_row + CHUNK, h * HEAD_DIM : (h + 1) * HEAD_DIM] = source[
+                h, first_row : first_row + CHUNK
+            ]
+        copy = pltpu.make_async_copy(
+            buf.at[pl.ds(buf_row, CHUNK)], target.at[pl.ds(target_row, CHUNK)], sems.at[n]
         )
-        copies.append(
-            pltpu.make_async_copy(
-                source.at[h, pl.ds(BLK, hb)],
-                narrow.at[pl.ds(half * hb, hb), head_cols(h)],
-                sems.at[2 * h + 1],
-            )
-        )
-    for copy in copies:
         copy.start()
+        copies.append(copy)
+
+    for r in range(0, BLK, CHUNK):
+        fill(wide_buf, wide, r, r, r, len(copies))
+    for r in range(0, hb, CHUNK):
+        fill(narrow_buf, narrow, BLK + r, r, half * hb + r, len(copies))
     for copy in copies:
         copy.wait()
 
 
-def own_kernel(sc_ref, own_ref, dq_ref, dk_ref, dv_ref, sems):
+def own_kernel(sc_ref, own_ref, dq_ref, dk_ref, dv_ref, *bufs):
     mine = own_ref.at[sc_ref[0]]
 
     @pl.when(sc_ref[1] == 1)
     def _():
-        put_pair(mine, dq_ref, dv_ref, 0, sems)
+        put_pair(mine, dq_ref, dv_ref, 0, *bufs)
 
     @pl.when(sc_ref[1] == 0)
     def _():
-        put_pair(mine, dk_ref, dv_ref, 1, sems)
-
-
-def other_kernel(sc_ref, got_ref, dq_in, dk_in, dv_in, dq_ref, dk_ref, dv_ref, sems):
+        put_pair(mine, dk_ref, dv_ref, 1, *bufs)
+
+
+def other_kernel(sc_ref, got_ref, dq_in, dk_in, dv_in, dq_ref, dk_ref, dv_ref, *bufs):
     del dq_in, dk_in, dv_in
 
     @pl.when(sc_ref[1] == 1)
     def _():
-        put_pair(got_ref, dk_ref, dv_ref, 1, sems)
+        put_pair(got_ref, dk_ref, dv_ref, 1, *bufs)
 
     @pl.when(sc_ref[1] == 0)
     def _():
-        put_pair(got_ref, dq_ref, dv_ref, 0, sems)
+        put_pair(got_ref, dq_ref, dv_ref, 0, *bufs)
 
 
 def place_call(kernel, name, scalars, part, so_far):
     shape = jax.ShapeDtypeStruct((BLK, HEADS * HEAD_DIM), jnp.bfloat16)
     return pl.pallas_call(
         kernel,
-        in_specs=[SMEM_SPEC, ANY_SPEC] + [HBM_SPEC] * len(so_far),
+        in_specs=[SMEM_SPEC, VMEM_SPEC] + [HBM_SPEC] * len(so_far),
         out_specs=[HBM_SPEC] * 3,
         out_shape=[shape] * 3,
         input_output_aliases={2 + i: i for i in range(len(so_far))},
-        scratch_shapes=[pltpu.SemaphoreType.DMA((2 * HEADS,))],
+        scratch_shapes=[
+            pltpu.VMEM((BLK, HEADS * HEAD_DIM), jnp.bfloat16),
+            pltpu.VMEM((BLK // 2, HEADS * HEAD_DIM), jnp.bfloat16),
+            pltpu.SemaphoreType.DMA((6,)),
+        ],
         cost_estimate=pl.CostEstimate(flops=0, transcendentals=0, bytes_accessed=4 * 2**20),
         compiler_params=pltpu.CompilerParams(vmem_limit_bytes=4 * 2**20),
         name=name,
@@ -304,11 +319,12 @@
         pltpu.with_memory_space_constraint(x, pltpu.HBM)
         for x in (queries, key_rows, value_rows, out_grad)
     )
-    sent = pair_call(sent_kernel, (), 4, "take_sent", scalars, *rows)
+    sent = pair_call(sent_kernel, "take_sent", scalars, *rows)
     got = lax.ppermute(sent, "core", SWAP)
-    kept = pair_call(kept_kernel, (2,), 60, "take_kept", scalars, *rows)
-    kept = lax.dynamic_update_slice(kept, got[None], (1 - core, 0, 0, 0, 0))
-    spread = kept.reshape(NBLOCKS, 2, BLK, HEAD_DIM)
+    kept = pair_call(kept_kernel, "take_kept", scalars, *rows)
+    own_document = jnp.arange(2, dtype=jnp.int32).reshape(2, 1, 1, 1, 1) == core
+    spread = jnp.where(own_document, kept[None], got[None])
+    spread = spread.reshape(NBLOCKS, 2, BLK, HEAD_DIM)
     arrived = lax.all_to_all(spread, ORDER, split_axis=0, concat_axis=0, tiled=True)
     arrived = arrived.reshape(2, HALF, 2, BLK, HEAD_DIM)
     far_keys = lax.dynamic_index_in_dim(arrived, 1 - core, 0, keepdims=False)

time: 152 us -> 151 us (level); the launches traced: 152 us -> 148 us
  Pallas kernels: 20.2 us -> 14.7 us
  starting transfers between devices: 29.3 us -> 31.2 us
  other arithmetic: 2.41 us -> 4.06 us
    pallas_call x1, Pallas kernels: 10.5 us -> 7.1 us  [attend_call(): pl.pallas_call(attend_kernel, in_specs=[SMEM_SPEC, SMEM_SPEC, VMEM_SPEC,...]
    pallas_call x2, Pallas kernels: 5.53 us -> 3.86 us  [pair_call(): pl.pallas_call(kernel, in_specs=[SMEM_SPEC] + [HBM_SPEC] * 4, out_specs=V...]
    select_n x0 -> x1, other arithmetic: none -> 1.61 us  [body(): spread = jnp.where(own_document, kept[None], got[None])]
  transfers between devices with their start and end apart: 6 -> 6, of which waited for: 5 -> 6; matrix products, arithmetic and copies ran while one was open for 2% -> 2% of each run, Pallas kernels for 3% -> 2%
where the time goes in v3:
time: 151 us; the launch traced here: 148 us
  blocking collectives  48.4 us (32%)
  waiting for transfers between devices  46.9 us (31%)
  starting transfers between devices  31.2 us (21%)
  Pallas kernels  14.7 us (10%)
  other arithmetic  4.06 us (3%)
  local copies, waits for them, and re-layouts  2.17 us (1%)
    all_to_all x1, blocking collectives, body(): lax.all_to_all(outgoing, ORDER, split_axis=0, concat_axis=0, tiled=True)  48.4 us
    all_to_all x1, waiting for transfers between devices, body(): lax.all_to_all(spread, ORDER, split_axis=0, concat_axis=0, tiled=True)  41.9 us
    ppermute x1, starting transfers between devices, body(): got = lax.ppermute(sent, 'core', SWAP)  8.78 us
    all_to_all x1, starting transfers between devices, body(): lax.all_to_all(spread, ORDER, split_axis=0, concat_axis=0, tiled=True)  7.65 us
    pallas_call x1, Pallas kernels, attend_call(): pl.pallas_call(attend_kernel, in_specs=[SMEM_SPEC, SMEM_SPEC, VMEM_SPEC,...  7.1 us
    ppermute x1, starting transfers between devices, body(): near_keys = lax.ppermute(far_keys, 'core', SWAP)  5.65 us
    ppermute x1, starting transfers between devices, body(): from_other = lax.ppermute(for_other, 'core', SWAP)  4.31 us
    pallas_call x2, Pallas kernels, pair_call(): pl.pallas_call(kernel, in_specs=[SMEM_SPEC] + [HBM_SPEC] * 4, out_specs=V...  3.86 us
  transfers between devices with their start and end apart: 6, of which 6 were waited for; matrix products, arithmetic and copies ran while one was open for 2% of the time, Pallas kernels for 2%

profile of v3, /device:TPU:1, one launch (start us, length us, event | category | flops | bytes accessed | tf_op | source)
XLA Modules:
  0.0 148.4 jit_solution(671191440398906436)
XLA Ops:
  0.7 1.9 %take_sent.1 = bf16[16,2,128,128]{3,2,1,0:T(8,128)(2,1)S(1)} custom-call(s32[2]{0:T(128)S(1)} %pad_add_fusion.4.sc_ref, bf16[128,2048]{1,0:T(8,128)(2,1)} %q_ref.3, bf16[128,2048]{1,0:T(8,128)(2,1)} %k_ref.3, bf16[128,2048]{1,0:T(8,128)(2,1)} %v_ref.3, bf16[128,2048]{1,0:T(8,128)(2,1)} %d_ref.3), custom_call_target="tpu_custom_call" | custom-call | bytes 4194304 | tf_op jit(solution)/shard_map/take_sent/pallas_call | solution.py:74
  2.6 8.8 %collective-permute-start.1 = (bf16[16,2,128,128]{3,2,1,0:T(8,128)(2,1)S(1)}, bf16[16,2,128,128]{3,2,1,0:T(8,128)(2,1)S(1)}, u32[]{:S(2)}, u32[]{:S(2)}) collective-permute-start(bf16[16,2,128,128]{3,2,1,0:T(8,128)(2,1)S(1)} %take_sent.1), channel_id=1, source_target_pairs={{0,1},{1,0},{2,3},{3,2},{4,5},{5,4},{6,7},{7,6},{8,9},{9,8},{10,11... | collective-permute-start | bytes 3145736 | tf_op jit(solution)/shard_map/ppermute | solution.py:323
  11.4 1.9 %take_kept.1 = bf16[16,2,128,128]{3,2,1,0:T(8,128)(2,1)S(1)} custom-call(s32[2]{0:T(128)S(1)} %pad_add_fusion.4.sc_ref, bf16[128,2048]{1,0:T(8,128)(2,1)} %q_ref.3, bf16[128,2048]{1,0:T(8,128)(2,1)} %k_ref.3, bf16[128,2048]{1,0:T(8,128)(2,1)} %v_ref.3, bf16[128,2048]{1,0:T(8,128)(2,1)} %d_ref.3), custom_call_target="tpu_custom_call" | custom-call | bytes 4194304 | tf_op jit(solution)/shard_map/take_kept/pallas_call | solution.py:74
  13.7 1.6 %bitcast_select_fusion = bf16[32,2,128,128]{3,2,1,0:T(8,128)(2,1)} fusion(pred[32]{0:T(512)(128)(4,1)S(1)} %broadcast_in_dim.92, bf16[16,2,128,128]{3,2,1,0:T(8,128)(2,1)S(1)} %collective-permute-done.1, bf16[16,2,128,128]{3,2,1,0:T(8,128)(2,1)S(1)} %take_kept.1), kind=kLoop, calls=%fused_computation | loop fusion | flops 1048576 | bytes 4194336 | tf_op jit(solution)/shard_map/jit(_where)/select_n | solution.py:326
  15.3 7.6 %all-to-all-start = ((bf16[32,2,128,128]{3,2,1,0:T(8,128)(2,1)}), bf16[32,2,128,128]{3,2,1,0:T(8,128)(2,1)S(1)}, u32[]{:S(2)}, u32[]{:S(2)}) async-start(bf16[32,2,128,128]{3,2,1,0:T(8,128)(2,1)} %bitcast_select_fusion), calls=%async_computation | async-start | bytes 4194304 | tf_op jit(solution)/shard_map/all_to_all | solution.py:328
  23.0 2.6 %collective-permute-start = (s32[16,14]{0,1:T(8,128)S(1)}, s32[16,14]{0,1:T(8,128)S(1)}, u32[]{:S(2)}, u32[]{:S(2)}) collective-permute-start(s32[16,14]{0,1:T(8,128)S(1)} %pad_add_fusion), channel_id=1, source_target_pairs={{0,1},{1,0},{2,3},{3,2},{4,5},{5,4},{6,7},{7,6},{8,9},{9,8},{10,11... | collective-permute-start | bytes 2696 | tf_op jit(solution)/shard_map/ppermute | solution.py:313
  25.6 0.8 collective-permute-done
  26.5 0.5 fusion.9
  27.0 0.6 iota_compare_fusion.4
  27.7 0.7 iota_compare_fusion.5
  28.6 41.9 %all-to-all-done = bf16[32,2,128,128]{3,2,1,0:T(8,128)(2,1)S(1)} async-done(((bf16[32,2,128,128]{3,2,1,0:T(8,128)(2,1)}), bf16[32,2,128,128]{3,2,1,0:T(8,128)(2,1)S(1)}, u32[]{:S(2)}, u32[]{:S(2)}) %all-to-all-start) | async-done | bytes 2097184 | tf_op jit(solution)/shard_map/all_to_all | solution.py:328
  70.5 1.1 dynamic-slice_bitcast_fusion
  71.6 5.7 %collective-permute-start.2 = (bf16[16,2,128,128]{3,2,1,0:T(8,128)(2,1)}, bf16[16,2,128,128]{3,2,1,0:T(8,128)(2,1)S(1)}, u32[]{:S(2)}, u32[]{:S(2)}) collective-permute-start(bf16[16,2,128,128]{3,2,1,0:T(8,128)(2,1)} %dynamic-slice_bitcast_fusion), channel_id=1, source_target_pairs={{0,1},{1,0},{2,3},{3,2},{4,5},{5,4},{6,7},{7,6},{8,9},{9,8},{10,11... | collective-permute-start | bytes 3145736 | tf_op jit(solution)/shard_map/ppermute | solution.py:331
  77.5 0.2 convert_reduce_fusion
  78.3 1.5 collective-permute-done.2.z_ref
  79.7 7.1 %attend.1 = (bf16[16,128,128]{2,1,0:T(8,128)(2,1)S(1)}, bf16[16,256,128]{2,1,0:T(8,128)(2,1)S(1)}, f32[16,256,128]{2,1,0:T(8,128)S(1)}) custom-call(s32[2]{0:T(128)S(1)} %pad_add_fusion.4.sc_ref, s32[16,14]{1,0:T(8,128)S(1)} %pad_add_fusion.2.tab_ref, bf16[2,16,2,128,128]{4,3,2,1,0:T(8,128)(2,1)S(1)} %bitcast.18, ...), custom_call_target="tpu_custom_call" | custom-call | tf_op jit(solution)/shard_map/attend/pallas_call | solution.py:169
  86.8 2.3 %collective-permute-start.3 = (bf16[16,256,128]{2,1,0:T(8,128)(2,1)S(1)}, bf16[16,256,128]{2,1,0:T(8,128)(2,1)S(1)}, u32[]{:S(2)}, u32[]{:S(2)}) collective-permute-start(bf16[16,256,128]{2,1,0:T(8,128)(2,1)S(1)} %get-tuple-element.11), channel_id=1, source_target_pairs={{0,1},{1,0},{2,3},{3,2},{4,5},{5,4},{6,7},{7,6},{8,9},{9,8},{10,11... | collective-permute-start | bytes 3145736 | tf_op jit(solution)/shard_map/ppermute | solution.py:334
  89.1 2.3 %collective-permute-done.3.got_ref = bf16[16,256,128]{2,1,0:T(8,128)(2,1)S(1)} collective-permute-done((bf16[16,256,128]{2,1,0:T(8,128)(2,1)S(1)}, bf16[16,256,128]{2,1,0:T(8,128)(2,1)S(1)}, u32[]{:S(2)}, u32[]{:S(2)}) %collective-permute-start.3) | collective-permute-done | bytes 1048608 | tf_op jit(solution)/shard_map/ppermute | solution.py:334
  91.4 0.7 join_partials.1
  92.2 48.4 %all_to_all.10 = bf16[32,192,128]{2,1,0:T(8,128)(2,1)S(1)} all-to-all(bf16[32,192,128]{2,1,0:T(8,128)(2,1)S(1)} %bitcast.21), channel_id=1, replica_groups=mesh['x'=4,'zh'=4,'zl'=2,'y'=8,'core'=2] {'zl','x','zh'}, dimensions={0} | all-to-all | bytes 3145728 | tf_op jit(solution)/shard_map/all_to_all | solution.py:337
  140.6 4.3 %collective-permute-start.4 = (bf16[16,192,128]{2,1,0:T(8,128)(2,1)S(1)}, bf16[16,192,128]{2,1,0:T(8,128)(2,1)S(1)}, u32[]{:S(2)}, u32[]{:S(2)}) collective-permute-start(bf16[16,192,128]{2,1,0:T(8,128)(2,1)S(1)} %dynamic-slice_bitcast_fusion.1), channel_id=1, source_target_pairs={{0,1},{1,0},{2,3},{3,2},{4,5},{5,4},{6,7},{7,6},{8,9},{9,8},{10,11... | collective-permute-start | bytes 2359304 | tf_op jit(solution)/shard_map/ppermute | solution.py:340
  144.9 1.5 %place_own.1 = (bf16[128,2048]{1,0:T(8,128)(2,1)}, bf16[128,2048]{1,0:T(8,128)(2,1)}, bf16[128,2048]{1,0:T(8,128)(2,1)}) custom-call(s32[2]{0:T(128)S(1)} %pad_add_fusion.4.sc_ref, bf16[2,16,192,128]{3,2,1,0:T(8,128)(2,1)S(1)} %bitcast.20), custom_call_target="tpu_custom_call" | custom-call | bytes 4194304 | tf_op jit(solution)/shard_map/place_own/pallas_call | solution.py:258
  146.4 0.4 collective-permute-done.4.got_ref
  146.8 1.5 %place_other.1 = (bf16[128,2048]{1,0:T(8,128)(2,1)}, bf16[128,2048]{1,0:T(8,128)(2,1)}, bf16[128,2048]{1,0:T(8,128)(2,1)}) custom-call(s32[2]{0:T(128)S(1)} %pad_add_fusion.4.sc_ref, bf16[16,192,128]{2,1,0:T(8,128)(2,1)S(1)} %collective-permute-done.4.got_ref, ...), custom_call_target="tpu_custom_call", output_to_operand_aliasing={{0}: (2, {}), {1}: (3, {}), {2}: (4, {})} | custom-call | bytes 4194304 | tf_op jit(solution)/shard_map/place_other/pallas_call | solution.py:258
  (30 shorter events, 1.7 us)
Async XLA Ops:
  2.6 11.1 %collective-permute-start.1 = (bf16[16,2,128,128]{3,2,1,0:T(8,128)(2,1)S(1)}, bf16[16,2,128,128]{3,2,1,0:T(8,128)(2,1)S(1)}, u32[]{:S(2)}, u32[]{:S(2)}) collective-permute-start(bf16[16,2,128,128]{3,2,1,0:T(8,128)(2,1)S(1)} %take_sent.1), channel_id=1, source_target_pairs={{0,1},{1,0},{2,3},{3,2},{4,5},{5,4},{6,7},{7,6},{8,9},{9,8},{10,11... | collective-permute-start | bytes 3145736 | tf_op jit(solution)/shard_map/ppermute | solution.py:323
  15.3 7.7 %copy-start = (s32[16,6]{0,1:T(8,128)S(1)}, s32[16,6]{0,1:T(8,128)}, u32[]{:S(2)}) copy-start(s32[16,6]{0,1:T(8,128)} %param.12) | copy-start | bytes 1156
  15.3 7.7 %copy-start.1 = (s32[16,6]{0,1:T(8,128)S(1)}, s32[16,6]{0,1:T(8,128)}, u32[]{:S(2)}) copy-start(s32[16,6]{0,1:T(8,128)} %param.11) | copy-start | bytes 1156
  15.3 7.7 %copy-start.2 = (s32[16,2]{0,1:T(2,128)S(1)}, s32[16,2]{0,1:T(2,128)}, u32[]{:S(2)}) copy-start(s32[16,2]{0,1:T(2,128)} %param.13) | copy-start | bytes 388
  15.3 55.2 %all-to-all-start = ((bf16[32,2,128,128]{3,2,1,0:T(8,128)(2,1)}), bf16[32,2,128,128]{3,2,1,0:T(8,128)(2,1)S(1)}, u32[]{:S(2)}, u32[]{:S(2)}) async-start(bf16[32,2,128,128]{3,2,1,0:T(8,128)(2,1)} %bitcast_select_fusion), calls=%async_computation | async-start | bytes 4194304 | tf_op jit(solution)/shard_map/all_to_all | solution.py:328
  23.0 3.4 %collective-permute-start = (s32[16,14]{0,1:T(8,128)S(1)}, s32[16,14]{0,1:T(8,128)S(1)}, u32[]{:S(2)}, u32[]{:S(2)}) collective-permute-start(s32[16,14]{0,1:T(8,128)S(1)} %pad_add_fusion), channel_id=1, source_target_pairs={{0,1},{1,0},{2,3},{3,2},{4,5},{5,4},{6,7},{7,6},{8,9},{9,8},{10,11... | collective-permute-start | bytes 2696 | tf_op jit(solution)/shard_map/ppermute | solution.py:313
  71.6 8.1 %collective-permute-start.2 = (bf16[16,2,128,128]{3,2,1,0:T(8,128)(2,1)}, bf16[16,2,128,128]{3,2,1,0:T(8,128)(2,1)S(1)}, u32[]{:S(2)}, u32[]{:S(2)}) collective-permute-start(bf16[16,2,128,128]{3,2,1,0:T(8,128)(2,1)} %dynamic-slice_bitcast_fusion), channel_id=1, source_target_pairs={{0,1},{1,0},{2,3},{3,2},{4,5},{5,4},{6,7},{7,6},{8,9},{9,8},{10,11... | collective-permute-start | bytes 3145736 | tf_op jit(solution)/shard_map/ppermute | solution.py:331
  86.8 4.6 %collective-permute-start.3 = (bf16[16,256,128]{2,1,0:T(8,128)(2,1)S(1)}, bf16[16,256,128]{2,1,0:T(8,128)(2,1)S(1)}, u32[]{:S(2)}, u32[]{:S(2)}) collective-permute-start(bf16[16,256,128]{2,1,0:T(8,128)(2,1)S(1)} %get-tuple-element.11), channel_id=1, source_target_pairs={{0,1},{1,0},{2,3},{3,2},{4,5},{5,4},{6,7},{7,6},{8,9},{9,8},{10,11... | collective-permute-start | bytes 3145736 | tf_op jit(solution)/shard_map/ppermute | solution.py:334
  140.6 6.2 %collective-permute-start.4 = (bf16[16,192,128]{2,1,0:T(8,128)(2,1)S(1)}, bf16[16,192,128]{2,1,0:T(8,128)(2,1)S(1)}, u32[]{:S(2)}, u32[]{:S(2)}) collective-permute-start(bf16[16,192,128]{2,1,0:T(8,128)(2,1)S(1)} %dynamic-slice_bitcast_fusion.1), channel_id=1, source_target_pairs={{0,1},{1,0},{2,3},{3,2},{4,5},{5,4},{6,7},{7,6},{8,9},{9,8},{10,11... | collective-permute-start | bytes 2359304 | tf_op jit(solution)/shard_map/ppermute | solution.py:340

commit v4 on v3

--- a/solution.py
+++ b/solution.py
@@ -14,7 +14,7 @@
 NBLOCKS = 32
 HALF = NBLOCKS // 2
 SLOTS = 12
-TOGETHER = 4
+TOGETHER = 8
 SCALE = HEAD_DIM ** (-0.5)
 ORDER = ("zl", "x", "zh")
 SWAP = [(0, 1), (1, 0)]
@@ -113,8 +113,9 @@
             @pl.when(pairs == groups)
             def _(groups=groups):
                 slots = range(2 * groups)
-                scored = []
-                for m, count in zip(rows, counts):
+
+                def score(r):
+                    m, count = rows[r], counts[r]
                     q = y_ref[core, m, 0]
                     d = y_ref[core, m, 1]
                     places = [tab_ref[m, a] for a in slots]
@@ -129,9 +130,9 @@
                         ],
                         axis=0,
                     )
-                    scored.append((m, q, d, places, k_rows, s, g))
-                formed = []
-                for m, q, d, places, k_rows, s, g in scored:
+                    return m, q, d, places, k_rows, s, g
+
+                def form(m, q, d, places, k_rows, s, g):
                     top = jnp.max(s, axis=0, keepdims=True)
                     e = jnp.exp((s - top) * SCALE)
                     inverse = 1.0 / jnp.sum(e, axis=0, keepdims=True)
@@ -139,8 +140,9 @@
                     p = e * inverse
                     w = p.astype(jnp.bfloat16)
                     ds = (p * (g - delta)).astype(jnp.bfloat16)
-                    formed.append((m, q, d, places, k_rows, w, ds))
-                for m, q, d, places, k_rows, w, ds in formed:
+                    return m, q, d, places, k_rows, w, ds
+
+                def spread(m, q, d, places, k_rows, w, ds):
                     for_keys = jnp.dot(ds, q, preferred_element_type=jnp.float32)
                     for_values = jnp.dot(w, d, preferred_element_type=jnp.float32)
                     for a in slots:
@@ -151,6 +153,15 @@
                         ds, k_rows, (((0,), (0,)), ((), ())), preferred_element_type=jnp.float32
                     )
                     dq_ref[m] = (dq * SCALE).astype(jnp.bfloat16)
+
+                scored, formed = {}, {}
+                for step_now in range(TOGETHER + 2):
+                    if step_now < TOGETHER:
+                        scored[step_now] = score(step_now)
+                    if 0 <= step_now - 1 < TOGETHER:
+                        formed[step_now - 1] = form(*scored.pop(step_now - 1))
+                    if step_now >= 2:
+                        spread(*formed.pop(step_now - 2))
 
     hb = BLK // 2
 

time: 151 us -> 151 us (level)
  no operation moved by 1% of the time
where the time goes in v4:
time: 151 us; the launch traced here: 149 us
  blocking collectives  49.4 us (33%)
  waiting for transfers between devices  46.9 us (31%)
  starting transfers between devices  31.2 us (21%)
  Pallas kernels  14 us (9%)
  other arithmetic  4.06 us (3%)
  local copies, waits for them, and re-layouts  2.17 us (1%)
    all_to_all x1, blocking collectives, body(): lax.all_to_all(outgoing, ORDER, split_axis=0, concat_axis=0, tiled=True)  49.4 us
    all_to_all x1, waiting for transfers between devices, body(): lax.all_to_all(spread, ORDER, split_axis=0, concat_axis=0, tiled=True)  41.9 us
    ppermute x1, starting transfers between devices, body(): got = lax.ppermute(sent, 'core', SWAP)  8.78 us
    all_to_all x1, starting transfers between devices, body(): lax.all_to_all(spread, ORDER, split_axis=0, concat_axis=0, tiled=True)  7.65 us
    pallas_call x1, Pallas kernels, attend_call(): pl.pallas_call(attend_kernel, in_specs=[SMEM_SPEC, SMEM_SPEC, VMEM_SPEC,...  6.39 us
    ppermute x1, starting transfers between devices, body(): near_keys = lax.ppermute(far_keys, 'core', SWAP)  5.65 us
    ppermute x1, starting transfers between devices, body(): from_other = lax.ppermute(for_other, 'core', SWAP)  4.31 us
    pallas_call x2, Pallas kernels, pair_call(): pl.pallas_call(kernel, in_specs=[SMEM_SPEC] + [HBM_SPEC] * 4, out_specs=V...  3.86 us
  transfers between devices with their start and end apart: 6, of which 6 were waited for; matrix products, arithmetic and copies ran while one was open for 2% of the time, Pallas kernels for 2%

profile of v4, /device:TPU:1, one launch (start us, length us, event | category | flops | bytes accessed | tf_op | source)
XLA Modules:
  0.0 148.8 jit_solution(11449677590953654301)
XLA Ops:
  0.7 1.9 %take_sent.1 = bf16[16,2,128,128]{3,2,1,0:T(8,128)(2,1)S(1)} custom-call(s32[2]{0:T(128)S(1)} %pad_add_fusion.4.sc_ref, bf16[128,2048]{1,0:T(8,128)(2,1)} %q_ref.3, bf16[128,2048]{1,0:T(8,128)(2,1)} %k_ref.3, bf16[128,2048]{1,0:T(8,128)(2,1)} %v_ref.3, bf16[128,2048]{1,0:T(8,128)(2,1)} %d_ref.3), custom_call_target="tpu_custom_call" | custom-call | bytes 4194304 | tf_op jit(solution)/shard_map/take_sent/pallas_call | solution.py:74
  2.6 8.8 %collective-permute-start.1 = (bf16[16,2,128,128]{3,2,1,0:T(8,128)(2,1)S(1)}, bf16[16,2,128,128]{3,2,1,0:T(8,128)(2,1)S(1)}, u32[]{:S(2)}, u32[]{:S(2)}) collective-permute-start(bf16[16,2,128,128]{3,2,1,0:T(8,128)(2,1)S(1)} %take_sent.1), channel_id=1, source_target_pairs={{0,1},{1,0},{2,3},{3,2},{4,5},{5,4},{6,7},{7,6},{8,9},{9,8},{10,11... | collective-permute-start | bytes 3145736 | tf_op jit(solution)/shard_map/ppermute | solution.py:334
  11.4 1.9 %take_kept.1 = bf16[16,2,128,128]{3,2,1,0:T(8,128)(2,1)S(1)} custom-call(s32[2]{0:T(128)S(1)} %pad_add_fusion.4.sc_ref, bf16[128,2048]{1,0:T(8,128)(2,1)} %q_ref.3, bf16[128,2048]{1,0:T(8,128)(2,1)} %k_ref.3, bf16[128,2048]{1,0:T(8,128)(2,1)} %v_ref.3, bf16[128,2048]{1,0:T(8,128)(2,1)} %d_ref.3), custom_call_target="tpu_custom_call" | custom-call | bytes 4194304 | tf_op jit(solution)/shard_map/take_kept/pallas_call | solution.py:74
  13.7 1.6 %bitcast_select_fusion = bf16[32,2,128,128]{3,2,1,0:T(8,128)(2,1)} fusion(pred[32]{0:T(512)(128)(4,1)S(1)} %broadcast_in_dim.92, bf16[16,2,128,128]{3,2,1,0:T(8,128)(2,1)S(1)} %collective-permute-done.1, bf16[16,2,128,128]{3,2,1,0:T(8,128)(2,1)S(1)} %take_kept.1), kind=kLoop, calls=%fused_computation | loop fusion | flops 1048576 | bytes 4194336 | tf_op jit(solution)/shard_map/jit(_where)/select_n | solution.py:337
  15.3 7.6 %all-to-all-start = ((bf16[32,2,128,128]{3,2,1,0:T(8,128)(2,1)}), bf16[32,2,128,128]{3,2,1,0:T(8,128)(2,1)S(1)}, u32[]{:S(2)}, u32[]{:S(2)}) async-start(bf16[32,2,128,128]{3,2,1,0:T(8,128)(2,1)} %bitcast_select_fusion), calls=%async_computation | async-start | bytes 4194304 | tf_op jit(solution)/shard_map/all_to_all | solution.py:339
  23.0 2.6 %collective-permute-start = (s32[16,14]{0,1:T(8,128)S(1)}, s32[16,14]{0,1:T(8,128)S(1)}, u32[]{:S(2)}, u32[]{:S(2)}) collective-permute-start(s32[16,14]{0,1:T(8,128)S(1)} %pad_add_fusion), channel_id=1, source_target_pairs={{0,1},{1,0},{2,3},{3,2},{4,5},{5,4},{6,7},{7,6},{8,9},{9,8},{10,11... | collective-permute-start | bytes 2696 | tf_op jit(solution)/shard_map/ppermute | solution.py:324
  25.6 0.8 collective-permute-done
  26.5 0.5 fusion.9
  27.0 0.6 iota_compare_fusion.4
  27.7 0.7 iota_compare_fusion.5
  28.6 41.9 %all-to-all-done = bf16[32,2,128,128]{3,2,1,0:T(8,128)(2,1)S(1)} async-done(((bf16[32,2,128,128]{3,2,1,0:T(8,128)(2,1)}), bf16[32,2,128,128]{3,2,1,0:T(8,128)(2,1)S(1)}, u32[]{:S(2)}, u32[]{:S(2)}) %all-to-all-start) | async-done | bytes 2097184 | tf_op jit(solution)/shard_map/all_to_all | solution.py:339
  70.5 1.1 dynamic-slice_bitcast_fusion
  71.6 5.7 %collective-permute-start.2 = (bf16[16,2,128,128]{3,2,1,0:T(8,128)(2,1)}, bf16[16,2,128,128]{3,2,1,0:T(8,128)(2,1)S(1)}, u32[]{:S(2)}, u32[]{:S(2)}) collective-permute-start(bf16[16,2,128,128]{3,2,1,0:T(8,128)(2,1)} %dynamic-slice_bitcast_fusion), channel_id=1, source_target_pairs={{0,1},{1,0},{2,3},{3,2},{4,5},{5,4},{6,7},{7,6},{8,9},{9,8},{10,11... | collective-permute-start | bytes 3145736 | tf_op jit(solution)/shard_map/ppermute | solution.py:342
  77.5 0.2 convert_reduce_fusion
  78.3 1.5 collective-permute-done.2.z_ref
  79.7 6.4 %attend.1 = (bf16[16,128,128]{2,1,0:T(8,128)(2,1)S(1)}, bf16[16,256,128]{2,1,0:T(8,128)(2,1)S(1)}, f32[16,256,128]{2,1,0:T(8,128)S(1)}) custom-call(s32[2]{0:T(128)S(1)} %pad_add_fusion.4.sc_ref, s32[16,14]{1,0:T(8,128)S(1)} %pad_add_fusion.2.tab_ref, bf16[2,16,2,128,128]{4,3,2,1,0:T(8,128)(2,1)S(1)} %bitcast.18, ...), custom_call_target="tpu_custom_call" | custom-call | tf_op jit(solution)/shard_map/attend/pallas_call | solution.py:180
  86.1 2.3 %collective-permute-start.3 = (bf16[16,256,128]{2,1,0:T(8,128)(2,1)S(1)}, bf16[16,256,128]{2,1,0:T(8,128)(2,1)S(1)}, u32[]{:S(2)}, u32[]{:S(2)}) collective-permute-start(bf16[16,256,128]{2,1,0:T(8,128)(2,1)S(1)} %get-tuple-element.11), channel_id=1, source_target_pairs={{0,1},{1,0},{2,3},{3,2},{4,5},{5,4},{6,7},{7,6},{8,9},{9,8},{10,11... | collective-permute-start | bytes 3145736 | tf_op jit(solution)/shard_map/ppermute | solution.py:345
  88.4 2.3 %collective-permute-done.3.got_ref = bf16[16,256,128]{2,1,0:T(8,128)(2,1)S(1)} collective-permute-done((bf16[16,256,128]{2,1,0:T(8,128)(2,1)S(1)}, bf16[16,256,128]{2,1,0:T(8,128)(2,1)S(1)}, u32[]{:S(2)}, u32[]{:S(2)}) %collective-permute-start.3) | collective-permute-done | bytes 1048608 | tf_op jit(solution)/shard_map/ppermute | solution.py:345
  90.7 0.7 join_partials.1
  91.4 49.4 %all_to_all.10 = bf16[32,192,128]{2,1,0:T(8,128)(2,1)S(1)} all-to-all(bf16[32,192,128]{2,1,0:T(8,128)(2,1)S(1)} %bitcast.21), channel_id=1, replica_groups=mesh['x'=4,'zh'=4,'zl'=2,'y'=8,'core'=2] {'zl','x','zh'}, dimensions={0} | all-to-all | bytes 3145728 | tf_op jit(solution)/shard_map/all_to_all | solution.py:348
  140.9 4.3 %collective-permute-start.4 = (bf16[16,192,128]{2,1,0:T(8,128)(2,1)S(1)}, bf16[16,192,128]{2,1,0:T(8,128)(2,1)S(1)}, u32[]{:S(2)}, u32[]{:S(2)}) collective-permute-start(bf16[16,192,128]{2,1,0:T(8,128)(2,1)S(1)} %dynamic-slice_bitcast_fusion.1), channel_id=1, source_target_pairs={{0,1},{1,0},{2,3},{3,2},{4,5},{5,4},{6,7},{7,6},{8,9},{9,8},{10,11... | collective-permute-start | bytes 2359304 | tf_op jit(solution)/shard_map/ppermute | solution.py:351
  145.2 1.5 %place_own.1 = (bf16[128,2048]{1,0:T(8,128)(2,1)}, bf16[128,2048]{1,0:T(8,128)(2,1)}, bf16[128,2048]{1,0:T(8,128)(2,1)}) custom-call(s32[2]{0:T(128)S(1)} %pad_add_fusion.4.sc_ref, bf16[2,16,192,128]{3,2,1,0:T(8,128)(2,1)S(1)} %bitcast.20), custom_call_target="tpu_custom_call" | custom-call | bytes 4194304 | tf_op jit(solution)/shard_map/place_own/pallas_call | solution.py:269
  146.7 0.4 collective-permute-done.4.got_ref
  147.1 1.5 %place_other.1 = (bf16[128,2048]{1,0:T(8,128)(2,1)}, bf16[128,2048]{1,0:T(8,128)(2,1)}, bf16[128,2048]{1,0:T(8,128)(2,1)}) custom-call(s32[2]{0:T(128)S(1)} %pad_add_fusion.4.sc_ref, bf16[16,192,128]{2,1,0:T(8,128)(2,1)S(1)} %collective-permute-done.4.got_ref, ...), custom_call_target="tpu_custom_call", output_to_operand_aliasing={{0}: (2, {}), {1}: (3, {}), {2}: (4, {})} | custom-call | bytes 4194304 | tf_op jit(solution)/shard_map/place_other/pallas_call | solution.py:269
  (30 shorter events, 1.7 us)
Async XLA Ops:
  2.6 11.1 %collective-permute-start.1 = (bf16[16,2,128,128]{3,2,1,0:T(8,128)(2,1)S(1)}, bf16[16,2,128,128]{3,2,1,0:T(8,128)(2,1)S(1)}, u32[]{:S(2)}, u32[]{:S(2)}) collective-permute-start(bf16[16,2,128,128]{3,2,1,0:T(8,128)(2,1)S(1)} %take_sent.1), channel_id=1, source_target_pairs={{0,1},{1,0},{2,3},{3,2},{4,5},{5,4},{6,7},{7,6},{8,9},{9,8},{10,11... | collective-permute-start | bytes 3145736 | tf_op jit(solution)/shard_map/ppermute | solution.py:334
  15.3 7.7 %copy-start = (s32[16,6]{0,1:T(8,128)S(1)}, s32[16,6]{0,1:T(8,128)}, u32[]{:S(2)}) copy-start(s32[16,6]{0,1:T(8,128)} %param.12) | copy-start | bytes 1156
  15.3 7.7 %copy-start.1 = (s32[16,6]{0,1:T(8,128)S(1)}, s32[16,6]{0,1:T(8,128)}, u32[]{:S(2)}) copy-start(s32[16,6]{0,1:T(8,128)} %param.11) | copy-start | bytes 1156
  15.3 7.7 %copy-start.2 = (s32[16,2]{0,1:T(2,128)S(1)}, s32[16,2]{0,1:T(2,128)}, u32[]{:S(2)}) copy-start(s32[16,2]{0,1:T(2,128)} %param.13) | copy-start | bytes 388
  15.3 55.2 %all-to-all-start = ((bf16[32,2,128,128]{3,2,1,0:T(8,128)(2,1)}), bf16[32,2,128,128]{3,2,1,0:T(8,128)(2,1)S(1)}, u32[]{:S(2)}, u32[]{:S(2)}) async-start(bf16[32,2,128,128]{3,2,1,0:T(8,128)(2,1)} %bitcast_select_fusion), calls=%async_computation | async-start | bytes 4194304 | tf_op jit(solution)/shard_map/all_to_all | solution.py:339
  23.0 3.4 %collective-permute-start = (s32[16,14]{0,1:T(8,128)S(1)}, s32[16,14]{0,1:T(8,128)S(1)}, u32[]{:S(2)}, u32[]{:S(2)}) collective-permute-start(s32[16,14]{0,1:T(8,128)S(1)} %pad_add_fusion), channel_id=1, source_target_pairs={{0,1},{1,0},{2,3},{3,2},{4,5},{5,4},{6,7},{7,6},{8,9},{9,8},{10,11... | collective-permute-start | bytes 2696 | tf_op jit(solution)/shard_map/ppermute | solution.py:324
  71.6 8.1 %collective-permute-start.2 = (bf16[16,2,128,128]{3,2,1,0:T(8,128)(2,1)}, bf16[16,2,128,128]{3,2,1,0:T(8,128)(2,1)S(1)}, u32[]{:S(2)}, u32[]{:S(2)}) collective-permute-start(bf16[16,2,128,128]{3,2,1,0:T(8,128)(2,1)} %dynamic-slice_bitcast_fusion), channel_id=1, source_target_pairs={{0,1},{1,0},{2,3},{3,2},{4,5},{5,4},{6,7},{7,6},{8,9},{9,8},{10,11... | collective-permute-start | bytes 3145736 | tf_op jit(solution)/shard_map/ppermute | solution.py:342
  86.1 4.6 %collective-permute-start.3 = (bf16[16,256,128]{2,1,0:T(8,128)(2,1)S(1)}, bf16[16,256,128]{2,1,0:T(8,128)(2,1)S(1)}, u32[]{:S(2)}, u32[]{:S(2)}) collective-permute-start(bf16[16,256,128]{2,1,0:T(8,128)(2,1)S(1)} %get-tuple-element.11), channel_id=1, source_target_pairs={{0,1},{1,0},{2,3},{3,2},{4,5},{5,4},{6,7},{7,6},{8,9},{9,8},{10,11... | collective-permute-start | bytes 3145736 | tf_op jit(solution)/shard_map/ppermute | solution.py:345
  140.9 6.2 %collective-permute-start.4 = (bf16[16,192,128]{2,1,0:T(8,128)(2,1)S(1)}, bf16[16,192,128]{2,1,0:T(8,128)(2,1)S(1)}, u32[]{:S(2)}, u32[]{:S(2)}) collective-permute-start(bf16[16,192,128]{2,1,0:T(8,128)(2,1)S(1)} %dynamic-slice_bitcast_fusion.1), channel_id=1, source_target_pairs={{0,1},{1,0},{2,3},{3,2},{4,5},{5,4},{6,7},{7,6},{8,9},{9,8},{10,11... | collective-permute-start | bytes 2359304 | tf_op jit(solution)/shard_map/ppermute | solution.py:351

commit v5 on v4

--- a/solution.py
+++ b/solution.py
@@ -16,7 +16,7 @@
 SLOTS = 12
 TOGETHER = 8
 SCALE = HEAD_DIM ** (-0.5)
-ORDER = ("zl", "x", "zh")
+ORDER = ("zl", "zh", "x")
 SWAP = [(0, 1), (1, 0)]
 NEG = -1e30
 VMEM_SPEC = pl.BlockSpec(memory_space=pltpu.VMEM)
@@ -283,8 +283,12 @@
     )(scalars, part, *so_far)
 
 
+def turned(m):
+    return ((m & 3) << 2) | ((m >> 2) & 3)
+
+
 def block_table(vert, slash, count, core):
-    chosen = core + 2 * jnp.arange(HALF, dtype=jnp.int32)
+    chosen = core + 2 * turned(jnp.arange(HALF, dtype=jnp.int32))
     vert_index = jnp.broadcast_to(vert[None, :], (HALF, vert.shape[0]))
     vert_valid = jnp.broadcast_to(
         (jnp.arange(vert.shape[0], dtype=jnp.int32) < count[0])[None, :], vert_index.shape
@@ -301,7 +305,7 @@
     )
     index = jnp.concatenate([vert_index, slash_index], axis=1)
     valid = jnp.concatenate([vert_valid, slash_valid], axis=1)
-    place = ((index & 1) ^ core) * HALF + (index >> 1)
+    place = ((index & 1) ^ core) * HALF + turned(index >> 1)
     rank = jnp.cumsum(valid.astype(jnp.int32), axis=1) - 1
     lanes = jnp.arange(SLOTS, dtype=jnp.int32)
     hit = valid[:, :, None] & (rank[:, :, None] == lanes[None, None, :])
@@ -317,7 +321,7 @@
 def body(queries, key_rows, value_rows, out_grad, vertical, slash_offsets, counts):
     core = lax.axis_index("core")
     parity = lax.axis_index("zl")
-    head = lax.axis_index("x") * lax.axis_size("zh") + lax.axis_index("zh")
+    head = lax.axis_index("zh") * lax.axis_size("x") + lax.axis_index("x")
     scalars = jnp.stack([core, (core == parity).astype(jnp.int32)]).astype(jnp.int32)
 
     tables = jnp.concatenate([vertical, slash_offsets, counts], axis=1)

time: 151 us -> 151 us (level)
  Pallas kernels: 14 us -> 16.3 us
  starting transfers between devices: 31.2 us -> 29 us
    pallas_call x1, Pallas kernels: 6.39 us -> 8.74 us  [attend_call(): pl.pallas_call(attend_kernel, in_specs=[SMEM_SPEC, SMEM_SPEC, VMEM_SPEC,...]
    ppermute x1, starting transfers between devices: 5.65 us -> 3.44 us  [body(): near_keys = lax.ppermute(far_keys, 'core', SWAP)]
where the time goes in v5:
time: 151 us; the launch traced here: 149 us
  waiting for transfers between devices  48.1 us (32%)
  blocking collectives  48 us (32%)
  starting transfers between devices  29 us (19%)
  Pallas kernels  16.3 us (11%)
  other arithmetic  4.06 us (3%)
  local copies, waits for them, and re-layouts  2.17 us (1%)
    all_to_all x1, blocking collectives, body(): lax.all_to_all(outgoing, ORDER, split_axis=0, concat_axis=0, tiled=True)  48 us
    all_to_all x1, waiting for transfers between devices, body(): lax.all_to_all(spread, ORDER, split_axis=0, concat_axis=0, tiled=True)  43.1 us
    ppermute x1, starting transfers between devices, body(): got = lax.ppermute(sent, 'core', SWAP)  8.78 us
    pallas_call x1, Pallas kernels, attend_call(): pl.pallas_call(attend_kernel, in_specs=[SMEM_SPEC, SMEM_SPEC, VMEM_SPEC,...  8.74 us
    all_to_all x1, starting transfers between devices, body(): lax.all_to_all(spread, ORDER, split_axis=0, concat_axis=0, tiled=True)  7.65 us
    ppermute x1, starting transfers between devices, body(): from_other = lax.ppermute(for_other, 'core', SWAP)  4.33 us
    pallas_call x2, Pallas kernels, pair_call(): pl.pallas_call(kernel, in_specs=[SMEM_SPEC] + [HBM_SPEC] * 4, out_specs=V...  3.86 us
    ppermute x1, starting transfers between devices, body(): near_keys = lax.ppermute(far_keys, 'core', SWAP)  3.44 us
  transfers between devices with their start and end apart: 6, of which 6 were waited for; matrix products, arithmetic and copies ran while one was open for 2% of the time, Pallas kernels for 2%

profile of v5, /device:TPU:1, one launch (start us, length us, event | category | flops | bytes accessed | tf_op | source)
XLA Modules:
  0.0 148.7 jit_solution(10707849322019140968)
XLA Ops:
  0.7 1.9 %take_sent.1 = bf16[16,2,128,128]{3,2,1,0:T(8,128)(2,1)S(1)} custom-call(s32[2]{0:T(128)S(1)} %pad_add_fusion.4.sc_ref, bf16[128,2048]{1,0:T(8,128)(2,1)} %q_ref.3, bf16[128,2048]{1,0:T(8,128)(2,1)} %k_ref.3, bf16[128,2048]{1,0:T(8,128)(2,1)} %v_ref.3, bf16[128,2048]{1,0:T(8,128)(2,1)} %d_ref.3), custom_call_target="tpu_custom_call" | custom-call | bytes 4194304 | tf_op jit(solution)/shard_map/take_sent/pallas_call | solution.py:74
  2.6 8.8 %collective-permute-start.1 = (bf16[16,2,128,128]{3,2,1,0:T(8,128)(2,1)S(1)}, bf16[16,2,128,128]{3,2,1,0:T(8,128)(2,1)S(1)}, u32[]{:S(2)}, u32[]{:S(2)}) collective-permute-start(bf16[16,2,128,128]{3,2,1,0:T(8,128)(2,1)S(1)} %take_sent.1), channel_id=1, source_target_pairs={{0,1},{1,0},{2,3},{3,2},{4,5},{5,4},{6,7},{7,6},{8,9},{9,8},{10,11... | collective-permute-start | bytes 3145736 | tf_op jit(solution)/shard_map/ppermute | solution.py:338
  11.4 1.9 %take_kept.1 = bf16[16,2,128,128]{3,2,1,0:T(8,128)(2,1)S(1)} custom-call(s32[2]{0:T(128)S(1)} %pad_add_fusion.4.sc_ref, bf16[128,2048]{1,0:T(8,128)(2,1)} %q_ref.3, bf16[128,2048]{1,0:T(8,128)(2,1)} %k_ref.3, bf16[128,2048]{1,0:T(8,128)(2,1)} %v_ref.3, bf16[128,2048]{1,0:T(8,128)(2,1)} %d_ref.3), custom_call_target="tpu_custom_call" | custom-call | bytes 4194304 | tf_op jit(solution)/shard_map/take_kept/pallas_call | solution.py:74
  13.7 1.6 %bitcast_select_fusion = bf16[32,2,128,128]{3,2,1,0:T(8,128)(2,1)} fusion(pred[32]{0:T(512)(128)(4,1)S(1)} %broadcast_in_dim.92, bf16[16,2,128,128]{3,2,1,0:T(8,128)(2,1)S(1)} %collective-permute-done.1, bf16[16,2,128,128]{3,2,1,0:T(8,128)(2,1)S(1)} %take_kept.1), kind=kLoop, calls=%fused_computation | loop fusion | flops 1048576 | bytes 4194336 | tf_op jit(solution)/shard_map/jit(_where)/select_n | solution.py:341
  15.3 7.6 %all-to-all-start = ((bf16[32,2,128,128]{3,2,1,0:T(8,128)(2,1)}), bf16[32,2,128,128]{3,2,1,0:T(8,128)(2,1)S(1)}, u32[]{:S(2)}, u32[]{:S(2)}) async-start(bf16[32,2,128,128]{3,2,1,0:T(8,128)(2,1)} %bitcast_select_fusion), calls=%async_computation | async-start | bytes 4194304 | tf_op jit(solution)/shard_map/all_to_all | solution.py:343
  23.0 2.6 %collective-permute-start = (s32[16,14]{0,1:T(8,128)S(1)}, s32[16,14]{0,1:T(8,128)S(1)}, u32[]{:S(2)}, u32[]{:S(2)}) collective-permute-start(s32[16,14]{0,1:T(8,128)S(1)} %pad_add_fusion), channel_id=1, source_target_pairs={{0,1},{1,0},{2,3},{3,2},{4,5},{5,4},{6,7},{7,6},{8,9},{9,8},{10,11... | collective-permute-start | bytes 2696 | tf_op jit(solution)/shard_map/ppermute | solution.py:328
  25.6 0.8 collective-permute-done
  26.5 0.5 fusion.19
  27.0 0.6 iota_compare_fusion.4
  27.7 0.7 iota_compare_fusion.5
  28.6 43.1 %all-to-all-done = bf16[32,2,128,128]{3,2,1,0:T(8,128)(2,1)S(1)} async-done(((bf16[32,2,128,128]{3,2,1,0:T(8,128)(2,1)}), bf16[32,2,128,128]{3,2,1,0:T(8,128)(2,1)S(1)}, u32[]{:S(2)}, u32[]{:S(2)}) %all-to-all-start) | async-done | bytes 2097184 | tf_op jit(solution)/shard_map/all_to_all | solution.py:343
  71.7 1.1 dynamic-slice_bitcast_fusion
  72.8 3.4 %collective-permute-start.2 = (bf16[16,2,128,128]{3,2,1,0:T(8,128)(2,1)}, bf16[16,2,128,128]{3,2,1,0:T(8,128)(2,1)S(1)}, u32[]{:S(2)}, u32[]{:S(2)}) collective-permute-start(bf16[16,2,128,128]{3,2,1,0:T(8,128)(2,1)} %dynamic-slice_bitcast_fusion), channel_id=1, source_target_pairs={{0,1},{1,0},{2,3},{3,2},{4,5},{5,4},{6,7},{7,6},{8,9},{9,8},{10,11... | collective-permute-start | bytes 3145736 | tf_op jit(solution)/shard_map/ppermute | solution.py:346
  76.5 0.2 convert_reduce_fusion
  77.2 1.5 collective-permute-done.2.z_ref
  78.7 8.7 %attend.1 = (bf16[16,128,128]{2,1,0:T(8,128)(2,1)S(1)}, bf16[16,256,128]{2,1,0:T(8,128)(2,1)S(1)}, f32[16,256,128]{2,1,0:T(8,128)S(1)}) custom-call(s32[2]{0:T(128)S(1)} %pad_add_fusion.4.sc_ref, s32[16,14]{1,0:T(8,128)S(1)} %pad_add_fusion.2.tab_ref, bf16[2,16,2,128,128]{4,3,2,1,0:T(8,128)(2,1)S(1)} %bitcast.18, ...), custom_call_target="tpu_custom_call" | custom-call | tf_op jit(solution)/shard_map/attend/pallas_call | solution.py:180
  87.5 2.3 %collective-permute-start.3 = (bf16[16,256,128]{2,1,0:T(8,128)(2,1)S(1)}, bf16[16,256,128]{2,1,0:T(8,128)(2,1)S(1)}, u32[]{:S(2)}, u32[]{:S(2)}) collective-permute-start(bf16[16,256,128]{2,1,0:T(8,128)(2,1)S(1)} %get-tuple-element.11), channel_id=1, source_target_pairs={{0,1},{1,0},{2,3},{3,2},{4,5},{5,4},{6,7},{7,6},{8,9},{9,8},{10,11... | collective-permute-start | bytes 3145736 | tf_op jit(solution)/shard_map/ppermute | solution.py:349
  89.7 2.3 %collective-permute-done.3.got_ref = bf16[16,256,128]{2,1,0:T(8,128)(2,1)S(1)} collective-permute-done((bf16[16,256,128]{2,1,0:T(8,128)(2,1)S(1)}, bf16[16,256,128]{2,1,0:T(8,128)(2,1)S(1)}, u32[]{:S(2)}, u32[]{:S(2)}) %collective-permute-start.3) | collective-permute-done | bytes 1048608 | tf_op jit(solution)/shard_map/ppermute | solution.py:349
  92.0 0.7 join_partials.1
  92.8 48.0 %all_to_all.10 = bf16[32,192,128]{2,1,0:T(8,128)(2,1)S(1)} all-to-all(bf16[32,192,128]{2,1,0:T(8,128)(2,1)S(1)} %bitcast.21), channel_id=1, replica_groups=mesh['x'=4,'zh'=4,'zl'=2,'y'=8,'core'=2] {'zl','zh','x'}, dimensions={0} | all-to-all | bytes 3145728 | tf_op jit(solution)/shard_map/all_to_all | solution.py:352
  140.8 4.3 %collective-permute-start.4 = (bf16[16,192,128]{2,1,0:T(8,128)(2,1)S(1)}, bf16[16,192,128]{2,1,0:T(8,128)(2,1)S(1)}, u32[]{:S(2)}, u32[]{:S(2)}) collective-permute-start(bf16[16,192,128]{2,1,0:T(8,128)(2,1)S(1)} %dynamic-slice_bitcast_fusion.1), channel_id=1, source_target_pairs={{0,1},{1,0},{2,3},{3,2},{4,5},{5,4},{6,7},{7,6},{8,9},{9,8},{10,11... | collective-permute-start | bytes 2359304 | tf_op jit(solution)/shard_map/ppermute | solution.py:355
  145.2 1.5 %place_own.1 = (bf16[128,2048]{1,0:T(8,128)(2,1)}, bf16[128,2048]{1,0:T(8,128)(2,1)}, bf16[128,2048]{1,0:T(8,128)(2,1)}) custom-call(s32[2]{0:T(128)S(1)} %pad_add_fusion.4.sc_ref, bf16[2,16,192,128]{3,2,1,0:T(8,128)(2,1)S(1)} %bitcast.20), custom_call_target="tpu_custom_call" | custom-call | bytes 4194304 | tf_op jit(solution)/shard_map/place_own/pallas_call | solution.py:269
  146.7 0.4 collective-permute-done.4.got_ref
  147.1 1.5 %place_other.1 = (bf16[128,2048]{1,0:T(8,128)(2,1)}, bf16[128,2048]{1,0:T(8,128)(2,1)}, bf16[128,2048]{1,0:T(8,128)(2,1)}) custom-call(s32[2]{0:T(128)S(1)} %pad_add_fusion.4.sc_ref, bf16[16,192,128]{2,1,0:T(8,128)(2,1)S(1)} %collective-permute-done.4.got_ref, ...), custom_call_target="tpu_custom_call", output_to_operand_aliasing={{0}: (2, {}), {1}: (3, {}), {2}: (4, {})} | custom-call | bytes 4194304 | tf_op jit(solution)/shard_map/place_other/pallas_call | solution.py:269
  (30 shorter events, 1.7 us)
Async XLA Ops:
  2.6 11.1 %collective-permute-start.1 = (bf16[16,2,128,128]{3,2,1,0:T(8,128)(2,1)S(1)}, bf16[16,2,128,128]{3,2,1,0:T(8,128)(2,1)S(1)}, u32[]{:S(2)}, u32[]{:S(2)}) collective-permute-start(bf16[16,2,128,128]{3,2,1,0:T(8,128)(2,1)S(1)} %take_sent.1), channel_id=1, source_target_pairs={{0,1},{1,0},{2,3},{3,2},{4,5},{5,4},{6,7},{7,6},{8,9},{9,8},{10,11... | collective-permute-start | bytes 3145736 | tf_op jit(solution)/shard_map/ppermute | solution.py:338
  15.3 7.7 %copy-start = (s32[16,6]{0,1:T(8,128)S(1)}, s32[16,6]{0,1:T(8,128)}, u32[]{:S(2)}) copy-start(s32[16,6]{0,1:T(8,128)} %param.12) | copy-start | bytes 1156
  15.3 7.7 %copy-start.1 = (s32[16,6]{0,1:T(8,128)S(1)}, s32[16,6]{0,1:T(8,128)}, u32[]{:S(2)}) copy-start(s32[16,6]{0,1:T(8,128)} %param.11) | copy-start | bytes 1156
  15.3 7.7 %copy-start.2 = (s32[16,2]{0,1:T(2,128)S(1)}, s32[16,2]{0,1:T(2,128)}, u32[]{:S(2)}) copy-start(s32[16,2]{0,1:T(2,128)} %param.13) | copy-start | bytes 388
  15.3 56.4 %all-to-all-start = ((bf16[32,2,128,128]{3,2,1,0:T(8,128)(2,1)}), bf16[32,2,128,128]{3,2,1,0:T(8,128)(2,1)S(1)}, u32[]{:S(2)}, u32[]{:S(2)}) async-start(bf16[32,2,128,128]{3,2,1,0:T(8,128)(2,1)} %bitcast_select_fusion), calls=%async_computation | async-start | bytes 4194304 | tf_op jit(solution)/shard_map/all_to_all | solution.py:343
  23.0 3.4 %collective-permute-start = (s32[16,14]{0,1:T(8,128)S(1)}, s32[16,14]{0,1:T(8,128)S(1)}, u32[]{:S(2)}, u32[]{:S(2)}) collective-permute-start(s32[16,14]{0,1:T(8,128)S(1)} %pad_add_fusion), channel_id=1, source_target_pairs={{0,1},{1,0},{2,3},{3,2},{4,5},{5,4},{6,7},{7,6},{8,9},{9,8},{10,11... | collective-permute-start | bytes 2696 | tf_op jit(solution)/shard_map/ppermute | solution.py:328
  72.8 5.9 %collective-permute-start.2 = (bf16[16,2,128,128]{3,2,1,0:T(8,128)(2,1)}, bf16[16,2,128,128]{3,2,1,0:T(8,128)(2,1)S(1)}, u32[]{:S(2)}, u32[]{:S(2)}) collective-permute-start(bf16[16,2,128,128]{3,2,1,0:T(8,128)(2,1)} %dynamic-slice_bitcast_fusion), channel_id=1, source_target_pairs={{0,1},{1,0},{2,3},{3,2},{4,5},{5,4},{6,7},{7,6},{8,9},{9,8},{10,11... | collective-permute-start | bytes 3145736 | tf_op jit(solution)/shard_map/ppermute | solution.py:346
  87.5 4.6 %collective-permute-start.3 = (bf16[16,256,128]{2,1,0:T(8,128)(2,1)S(1)}, bf16[16,256,128]{2,1,0:T(8,128)(2,1)S(1)}, u32[]{:S(2)}, u32[]{:S(2)}) collective-permute-start(bf16[16,256,128]{2,1,0:T(8,128)(2,1)S(1)} %get-tuple-element.11), channel_id=1, source_target_pairs={{0,1},{1,0},{2,3},{3,2},{4,5},{5,4},{6,7},{7,6},{8,9},{9,8},{10,11... | collective-permute-start | bytes 3145736 | tf_op jit(solution)/shard_map/ppermute | solution.py:349
  140.8 6.2 %collective-permute-start.4 = (bf16[16,192,128]{2,1,0:T(8,128)(2,1)S(1)}, bf16[16,192,128]{2,1,0:T(8,128)(2,1)S(1)}, u32[]{:S(2)}, u32[]{:S(2)}) collective-permute-start(bf16[16,192,128]{2,1,0:T(8,128)(2,1)S(1)} %dynamic-slice_bitcast_fusion.1), channel_id=1, source_target_pairs={{0,1},{1,0},{2,3},{3,2},{4,5},{5,4},{6,7},{7,6},{8,9},{9,8},{10,11... | collective-permute-start | bytes 2359304 | tf_op jit(solution)/shard_map/ppermute | solution.py:355

commit v6 on v5

--- a/solution.py
+++ b/solution.py
@@ -25,7 +25,7 @@
 SMEM_SPEC = pl.BlockSpec(memory_space=pltpu.SMEM)
 
 
-CHUNK = 32
+CHUNK = 16
 
 
 def take_pair(first, second, target, rows_buf, sems):
@@ -275,7 +275,7 @@
         scratch_shapes=[
             pltpu.VMEM((BLK, HEADS * HEAD_DIM), jnp.bfloat16),
             pltpu.VMEM((BLK // 2, HEADS * HEAD_DIM), jnp.bfloat16),
-            pltpu.SemaphoreType.DMA((6,)),
+            pltpu.SemaphoreType.DMA((12,)),
         ],
         cost_estimate=pl.CostEstimate(flops=0, transcendentals=0, bytes_accessed=4 * 2**20),
         compiler_params=pltpu.CompilerParams(vmem_limit_bytes=4 * 2**20),

time: 151 us -> 151 us (level); the launches traced: 149 us -> 150 us
  Pallas kernels: 16.3 us -> 18.9 us
    pallas_call x1, Pallas kernels: 8.74 us -> 11.2 us  [attend_call(): pl.pallas_call(attend_kernel, in_specs=[SMEM_SPEC, SMEM_SPEC, VMEM_SPEC,...]
where the time goes in v6:
time: 151 us; the launch traced here: 150 us
  waiting for transfers between devices  48.1 us (32%)
  blocking collectives  47.2 us (31%)
  starting transfers between devices  29 us (19%)
  Pallas kernels  18.9 us (13%)
  other arithmetic  4.06 us (3%)
  local copies, waits for them, and re-layouts  2.17 us (1%)
    all_to_all x1, blocking collectives, body(): lax.all_to_all(outgoing, ORDER, split_axis=0, concat_axis=0, tiled=True)  47.2 us
    all_to_all x1, waiting for transfers between devices, body(): lax.all_to_all(spread, ORDER, split_axis=0, concat_axis=0, tiled=True)  43.1 us
    pallas_call x1, Pallas kernels, attend_call(): pl.pallas_call(attend_kernel, in_specs=[SMEM_SPEC, SMEM_SPEC, VMEM_SPEC,...  11.2 us
    ppermute x1, starting transfers between devices, body(): got = lax.ppermute(sent, 'core', SWAP)  8.78 us
    all_to_all x1, starting transfers between devices, body(): lax.all_to_all(spread, ORDER, split_axis=0, concat_axis=0, tiled=True)  7.65 us
    ppermute x1, starting transfers between devices, body(): from_other = lax.ppermute(for_other, 'core', SWAP)  4.33 us
    pallas_call x2, Pallas kernels, pair_call(): pl.pallas_call(kernel, in_specs=[SMEM_SPEC] + [HBM_SPEC] * 4, out_specs=V...  3.88 us
    ppermute x1, starting transfers between devices, body(): near_keys = lax.ppermute(far_keys, 'core', SWAP)  3.44 us
  transfers between devices with their start and end apart: 6, of which 6 were waited for; matrix products, arithmetic and copies ran while one was open for 2% of the time, Pallas kernels for 2%

profile of v6, /device:TPU:1, one launch (start us, length us, event | category | flops | bytes accessed | tf_op | source)
XLA Modules:
  0.0 150.5 jit_solution(14496397448379017846)
XLA Ops:
  0.7 1.9 %take_sent.1 = bf16[16,2,128,128]{3,2,1,0:T(8,128)(2,1)S(1)} custom-call(s32[2]{0:T(128)S(1)} %pad_add_fusion.4.sc_ref, bf16[128,2048]{1,0:T(8,128)(2,1)} %q_ref.3, bf16[128,2048]{1,0:T(8,128)(2,1)} %k_ref.3, bf16[128,2048]{1,0:T(8,128)(2,1)} %v_ref.3, bf16[128,2048]{1,0:T(8,128)(2,1)} %d_ref.3), custom_call_target="tpu_custom_call" | custom-call | bytes 4194304 | tf_op jit(solution)/shard_map/take_sent/pallas_call | solution.py:74
  2.7 8.8 %collective-permute-start.1 = (bf16[16,2,128,128]{3,2,1,0:T(8,128)(2,1)S(1)}, bf16[16,2,128,128]{3,2,1,0:T(8,128)(2,1)S(1)}, u32[]{:S(2)}, u32[]{:S(2)}) collective-permute-start(bf16[16,2,128,128]{3,2,1,0:T(8,128)(2,1)S(1)} %take_sent.1), channel_id=1, source_target_pairs={{0,1},{1,0},{2,3},{3,2},{4,5},{5,4},{6,7},{7,6},{8,9},{9,8},{10,11... | collective-permute-start | bytes 3145736 | tf_op jit(solution)/shard_map/ppermute | solution.py:338
  11.5 1.9 %take_kept.1 = bf16[16,2,128,128]{3,2,1,0:T(8,128)(2,1)S(1)} custom-call(s32[2]{0:T(128)S(1)} %pad_add_fusion.4.sc_ref, bf16[128,2048]{1,0:T(8,128)(2,1)} %q_ref.3, bf16[128,2048]{1,0:T(8,128)(2,1)} %k_ref.3, bf16[128,2048]{1,0:T(8,128)(2,1)} %v_ref.3, bf16[128,2048]{1,0:T(8,128)(2,1)} %d_ref.3), custom_call_target="tpu_custom_call" | custom-call | bytes 4194304 | tf_op jit(solution)/shard_map/take_kept/pallas_call | solution.py:74
  13.7 1.6 %bitcast_select_fusion = bf16[32,2,128,128]{3,2,1,0:T(8,128)(2,1)} fusion(pred[32]{0:T(512)(128)(4,1)S(1)} %broadcast_in_dim.92, bf16[16,2,128,128]{3,2,1,0:T(8,128)(2,1)S(1)} %collective-permute-done.1, bf16[16,2,128,128]{3,2,1,0:T(8,128)(2,1)S(1)} %take_kept.1), kind=kLoop, calls=%fused_computation | loop fusion | flops 1048576 | bytes 4194336 | tf_op jit(solution)/shard_map/jit(_where)/select_n | solution.py:341
  15.3 7.6 %all-to-all-start = ((bf16[32,2,128,128]{3,2,1,0:T(8,128)(2,1)}), bf16[32,2,128,128]{3,2,1,0:T(8,128)(2,1)S(1)}, u32[]{:S(2)}, u32[]{:S(2)}) async-start(bf16[32,2,128,128]{3,2,1,0:T(8,128)(2,1)} %bitcast_select_fusion), calls=%async_computation | async-start | bytes 4194304 | tf_op jit(solution)/shard_map/all_to_all | solution.py:343
  23.0 2.6 %collective-permute-start = (s32[16,14]{0,1:T(8,128)S(1)}, s32[16,14]{0,1:T(8,128)S(1)}, u32[]{:S(2)}, u32[]{:S(2)}) collective-permute-start(s32[16,14]{0,1:T(8,128)S(1)} %pad_add_fusion), channel_id=1, source_target_pairs={{0,1},{1,0},{2,3},{3,2},{4,5},{5,4},{6,7},{7,6},{8,9},{9,8},{10,11... | collective-permute-start | bytes 2696 | tf_op jit(solution)/shard_map/ppermute | solution.py:328
  25.6 0.8 collective-permute-done
  26.5 0.5 fusion.19
  27.0 0.6 iota_compare_fusion.4
  27.7 0.7 iota_compare_fusion.5
  28.6 43.1 %all-to-all-done = bf16[32,2,128,128]{3,2,1,0:T(8,128)(2,1)S(1)} async-done(((bf16[32,2,128,128]{3,2,1,0:T(8,128)(2,1)}), bf16[32,2,128,128]{3,2,1,0:T(8,128)(2,1)S(1)}, u32[]{:S(2)}, u32[]{:S(2)}) %all-to-all-start) | async-done | bytes 2097184 | tf_op jit(solution)/shard_map/all_to_all | solution.py:343
  71.7 1.1 dynamic-slice_bitcast_fusion
  72.8 3.4 %collective-permute-start.2 = (bf16[16,2,128,128]{3,2,1,0:T(8,128)(2,1)}, bf16[16,2,128,128]{3,2,1,0:T(8,128)(2,1)S(1)}, u32[]{:S(2)}, u32[]{:S(2)}) collective-permute-start(bf16[16,2,128,128]{3,2,1,0:T(8,128)(2,1)} %dynamic-slice_bitcast_fusion), channel_id=1, source_target_pairs={{0,1},{1,0},{2,3},{3,2},{4,5},{5,4},{6,7},{7,6},{8,9},{9,8},{10,11... | collective-permute-start | bytes 3145736 | tf_op jit(solution)/shard_map/ppermute | solution.py:346
  76.5 0.2 convert_reduce_fusion
  77.3 1.5 collective-permute-done.2.z_ref
  78.7 11.2 %attend.1 = (bf16[16,128,128]{2,1,0:T(8,128)(2,1)S(1)}, bf16[16,256,128]{2,1,0:T(8,128)(2,1)S(1)}, f32[16,256,128]{2,1,0:T(8,128)S(1)}) custom-call(s32[2]{0:T(128)S(1)} %pad_add_fusion.4.sc_ref, s32[16,14]{1,0:T(8,128)S(1)} %pad_add_fusion.2.tab_ref, bf16[2,16,2,128,128]{4,3,2,1,0:T(8,128)(2,1)S(1)} %bitcast.18, ...), custom_call_target="tpu_custom_call" | custom-call | tf_op jit(solution)/shard_map/attend/pallas_call | solution.py:180
  90.0 2.3 %collective-permute-start.3 = (bf16[16,256,128]{2,1,0:T(8,128)(2,1)S(1)}, bf16[16,256,128]{2,1,0:T(8,128)(2,1)S(1)}, u32[]{:S(2)}, u32[]{:S(2)}) collective-permute-start(bf16[16,256,128]{2,1,0:T(8,128)(2,1)S(1)} %get-tuple-element.11), channel_id=1, source_target_pairs={{0,1},{1,0},{2,3},{3,2},{4,5},{5,4},{6,7},{7,6},{8,9},{9,8},{10,11... | collective-permute-start | bytes 3145736 | tf_op jit(solution)/shard_map/ppermute | solution.py:349
  92.3 2.3 %collective-permute-done.3.got_ref = bf16[16,256,128]{2,1,0:T(8,128)(2,1)S(1)} collective-permute-done((bf16[16,256,128]{2,1,0:T(8,128)(2,1)S(1)}, bf16[16,256,128]{2,1,0:T(8,128)(2,1)S(1)}, u32[]{:S(2)}, u32[]{:S(2)}) %collective-permute-start.3) | collective-permute-done | bytes 1048608 | tf_op jit(solution)/shard_map/ppermute | solution.py:349
  94.5 0.7 join_partials.1
  95.3 47.2 %all_to_all.10 = bf16[32,192,128]{2,1,0:T(8,128)(2,1)S(1)} all-to-all(bf16[32,192,128]{2,1,0:T(8,128)(2,1)S(1)} %bitcast.21), channel_id=1, replica_groups=mesh['x'=4,'zh'=4,'zl'=2,'y'=8,'core'=2] {'zl','zh','x'}, dimensions={0} | all-to-all | bytes 3145728 | tf_op jit(solution)/shard_map/all_to_all | solution.py:352
  142.5 4.3 %collective-permute-start.4 = (bf16[16,192,128]{2,1,0:T(8,128)(2,1)S(1)}, bf16[16,192,128]{2,1,0:T(8,128)(2,1)S(1)}, u32[]{:S(2)}, u32[]{:S(2)}) collective-permute-start(bf16[16,192,128]{2,1,0:T(8,128)(2,1)S(1)} %dynamic-slice_bitcast_fusion.1), channel_id=1, source_target_pairs={{0,1},{1,0},{2,3},{3,2},{4,5},{5,4},{6,7},{7,6},{8,9},{9,8},{10,11... | collective-permute-start | bytes 2359304 | tf_op jit(solution)/shard_map/ppermute | solution.py:355
  146.9 1.5 %place_own.1 = (bf16[128,2048]{1,0:T(8,128)(2,1)}, bf16[128,2048]{1,0:T(8,128)(2,1)}, bf16[128,2048]{1,0:T(8,128)(2,1)}) custom-call(s32[2]{0:T(128)S(1)} %pad_add_fusion.4.sc_ref, bf16[2,16,192,128]{3,2,1,0:T(8,128)(2,1)S(1)} %bitcast.20), custom_call_target="tpu_custom_call" | custom-call | bytes 4194304 | tf_op jit(solution)/shard_map/place_own/pallas_call | solution.py:269
  148.4 0.3 collective-permute-done.4.got_ref
  148.8 1.5 %place_other.1 = (bf16[128,2048]{1,0:T(8,128)(2,1)}, bf16[128,2048]{1,0:T(8,128)(2,1)}, bf16[128,2048]{1,0:T(8,128)(2,1)}) custom-call(s32[2]{0:T(128)S(1)} %pad_add_fusion.4.sc_ref, bf16[16,192,128]{2,1,0:T(8,128)(2,1)S(1)} %collective-permute-done.4.got_ref, ...), custom_call_target="tpu_custom_call", output_to_operand_aliasing={{0}: (2, {}), {1}: (3, {}), {2}: (4, {})} | custom-call | bytes 4194304 | tf_op jit(solution)/shard_map/place_other/pallas_call | solution.py:269
  (30 shorter events, 1.6 us)
Async XLA Ops:
  2.7 11.1 %collective-permute-start.1 = (bf16[16,2,128,128]{3,2,1,0:T(8,128)(2,1)S(1)}, bf16[16,2,128,128]{3,2,1,0:T(8,128)(2,1)S(1)}, u32[]{:S(2)}, u32[]{:S(2)}) collective-permute-start(bf16[16,2,128,128]{3,2,1,0:T(8,128)(2,1)S(1)} %take_sent.1), channel_id=1, source_target_pairs={{0,1},{1,0},{2,3},{3,2},{4,5},{5,4},{6,7},{7,6},{8,9},{9,8},{10,11... | collective-permute-start | bytes 3145736 | tf_op jit(solution)/shard_map/ppermute | solution.py:338
  15.3 7.7 %copy-start = (s32[16,6]{0,1:T(8,128)S(1)}, s32[16,6]{0,1:T(8,128)}, u32[]{:S(2)}) copy-start(s32[16,6]{0,1:T(8,128)} %param.12) | copy-start | bytes 1156
  15.3 7.7 %copy-start.1 = (s32[16,6]{0,1:T(8,128)S(1)}, s32[16,6]{0,1:T(8,128)}, u32[]{:S(2)}) copy-start(s32[16,6]{0,1:T(8,128)} %param.11) | copy-start | bytes 1156
  15.3 7.7 %copy-start.2 = (s32[16,2]{0,1:T(2,128)S(1)}, s32[16,2]{0,1:T(2,128)}, u32[]{:S(2)}) copy-start(s32[16,2]{0,1:T(2,128)} %param.13) | copy-start | bytes 388
  15.3 56.4 %all-to-all-start = ((bf16[32,2,128,128]{3,2,1,0:T(8,128)(2,1)}), bf16[32,2,128,128]{3,2,1,0:T(8,128)(2,1)S(1)}, u32[]{:S(2)}, u32[]{:S(2)}) async-start(bf16[32,2,128,128]{3,2,1,0:T(8,128)(2,1)} %bitcast_select_fusion), calls=%async_computation | async-start | bytes 4194304 | tf_op jit(solution)/shard_map/all_to_all | solution.py:343
  23.0 3.4 %collective-permute-start = (s32[16,14]{0,1:T(8,128)S(1)}, s32[16,14]{0,1:T(8,128)S(1)}, u32[]{:S(2)}, u32[]{:S(2)}) collective-permute-start(s32[16,14]{0,1:T(8,128)S(1)} %pad_add_fusion), channel_id=1, source_target_pairs={{0,1},{1,0},{2,3},{3,2},{4,5},{5,4},{6,7},{7,6},{8,9},{9,8},{10,11... | collective-permute-start | bytes 2696 | tf_op jit(solution)/shard_map/ppermute | solution.py:328
  72.8 5.9 %collective-permute-start.2 = (bf16[16,2,128,128]{3,2,1,0:T(8,128)(2,1)}, bf16[16,2,128,128]{3,2,1,0:T(8,128)(2,1)S(1)}, u32[]{:S(2)}, u32[]{:S(2)}) collective-permute-start(bf16[16,2,128,128]{3,2,1,0:T(8,128)(2,1)} %dynamic-slice_bitcast_fusion), channel_id=1, source_target_pairs={{0,1},{1,0},{2,3},{3,2},{4,5},{5,4},{6,7},{7,6},{8,9},{9,8},{10,11... | collective-permute-start | bytes 3145736 | tf_op jit(solution)/shard_map/ppermute | solution.py:346
  90.0 4.6 %collective-permute-start.3 = (bf16[16,256,128]{2,1,0:T(8,128)(2,1)S(1)}, bf16[16,256,128]{2,1,0:T(8,128)(2,1)S(1)}, u32[]{:S(2)}, u32[]{:S(2)}) collective-permute-start(bf16[16,256,128]{2,1,0:T(8,128)(2,1)S(1)} %get-tuple-element.11), channel_id=1, source_target_pairs={{0,1},{1,0},{2,3},{3,2},{4,5},{5,4},{6,7},{7,6},{8,9},{9,8},{10,11... | collective-permute-start | bytes 3145736 | tf_op jit(solution)/shard_map/ppermute | solution.py:349
  142.5 6.2 %collective-permute-start.4 = (bf16[16,192,128]{2,1,0:T(8,128)(2,1)S(1)}, bf16[16,192,128]{2,1,0:T(8,128)(2,1)S(1)}, u32[]{:S(2)}, u32[]{:S(2)}) collective-permute-start(bf16[16,192,128]{2,1,0:T(8,128)(2,1)S(1)} %dynamic-slice_bitcast_fusion.1), channel_id=1, source_target_pairs={{0,1},{1,0},{2,3},{3,2},{4,5},{5,4},{6,7},{7,6},{8,9},{9,8},{10,11... | collective-permute-start | bytes 2359304 | tf_op jit(solution)/shard_map/ppermute | solution.py:355
